TPU v7x, 32 devices: a whole 2x2x4 slice. The times are simulated.
32 devices in a mesh: dom: 8 (over y, x, core), st: 4 (over z).
Axes of the slice: x: 2, y: 2, z: 4, core: 2. Of those that a mesh axis runs over, the one named last changes fastest.
Arguments:
- start_block: bfloat16 [2, 64, 128, 729], P(None, 'dom', 'st'), may hold values from -48 to 48
- resident: bfloat16 [1024, 64, 729], P('st', 'dom'), may hold values from -0.09375 to 0.09375
- stiffness: bfloat16 [729, 729], replicated, may hold values from -0.21875 to 0.21875
- cell_scale: float32 [64], P('dom'), may hold values from 0.5 to 2
- potential: float32 [64, 729], P('dom'), may hold values from -1 to 1
- cell_count: int32 [8], P('dom'), may hold values from 2 to 8, as said below
- face_index: int32 [8, 2, 81], P('dom'), may hold values from 0 to 5831, as said below
Outputs:
- rotated: bfloat16 [2, 64, 128, 729], P(None, 'dom', 'st')
Inputs may be any that keep to these rules, and one draw needn't show every extreme that they name: Domain d has cell_count[d] live cells in its first slots; some domain has 8 and some has 2. face_index[d, 0, :] lists each node of the last face of domain d's last live cell once, face_index[d, 1, :] each node of the first face of its cell 0 once, as flat indices cell * 729 + node; the k-th entries of face_index[d, 0] and face_index[d + 1, 1] are the same mesh node.
All inputs are finite; a program needn't handle non-finite values.
Results may differ from a plain program's by a relative error of at most 0.0075.
Values may be sent and summed in bfloat16 or wider, within the bound.
A program may use at most 64 MiB of HBM per device.

v0:
```python
from functools import partial

import jax
import jax.numpy as jnp
from jax import lax
from jax.experimental import pallas as pl
from jax.experimental.pallas import tpu as pltpu
from jax.sharding import PartitionSpec as P

CENTER = 0.5
HALF_WIDTH = 2.0
EPSILON = 1e-06
F32 = jnp.float32
BF16 = jnp.bfloat16
RIGHT, LEFT = 0, 1


def dot_nn(a, b, precision=None):
    return lax.dot_general(
        a, b, (((1,), (0,)), ((), ())), precision=precision, preferred_element_type=F32
    )


def dot_nt(a, b, precision=None):
    return lax.dot_general(
        a, b, (((1,), (1,)), ((), ())), precision=precision, preferred_element_type=F32
    )


def kernel(
    sizes,
    scale_ref,
    count_ref,
    start_ref,
    res_hbm,
    stiff_ref,
    pot_ref,
    face_ref,
    out_ref,
    local,
    inner,
    states,
    part,
    part_recv,
    total,
    mix,
    proj,
    share,
    share_recv,
    res_in,
    res_wide,
    res_ref,
    res_near,
    proj_near,
    retained,
    face_out,
    face_in,
    face_send_sem,
    face_recv_sem,
    gather_send_sem,
    gather_recv_sem,
    one_send_sem,
    one_recv_sem,
    two_send_sem,
    two_recv_sem,
    share_send_sem,
    share_recv_sem,
    load_sem,
    near_send_sem,
    near_recv_sem,
    coef_send_sem,
    coef_recv_sem,
):
    doms, sts, blocks, cells, width, nodes, face, res, rows, moved = sizes
    total_states = sts * width
    total_nodes = float(doms * cells * nodes)
    window = (nodes - face) // 128 * 128
    offset = nodes - face - window
    d = lax.axis_index("dom")
    s = lax.axis_index("st")
    has_right, has_left = s < sts - 1, s > 0
    has_next, has_prev = d < doms - 1, d > 0
    own = pl.ds(pl.multiple_of(s * width, width), width)
    pending = []
    both = jnp.logical_and
    count = count_ref[0]
    scale = [scale_ref[c] for c in range(cells)]
    live = [jnp.where(c < count, 1.0, 0.0).astype(F32) for c in range(cells)]
    last = [jnp.where(c == count - 1, 1.0, 0.0).astype(F32) for c in range(cells)]
    load = pltpu.make_async_copy(res_hbm, res_in, load_sem)
    load.start()

    def dom_peer(k):
        return lax.rem(d + k, doms)

    barrier = pltpu.get_barrier_semaphore()

    def greet(k, carry):
        pl.semaphore_signal(
            barrier, inc=1, device_id={"dom": dom_peer(k)}, device_id_type=pl.DeviceIdType.MESH
        )
        return carry

    lax.fori_loop(1, doms, greet, 0)

    @pl.when(has_right)
    def _():
        pl.semaphore_signal(
            barrier, inc=1, device_id={"st": s + 1}, device_id_type=pl.DeviceIdType.MESH
        )

    @pl.when(has_left)
    def _():
        pl.semaphore_signal(
            barrier, inc=1, device_id={"st": s - 1}, device_id_type=pl.DeviceIdType.MESH
        )

    neighbours = has_right.astype(jnp.int32) + has_left.astype(jnp.int32)
    pl.semaphore_wait(barrier, doms - 1 + neighbours)

    def remote(src, dst, send_sem, recv_sem, axis, peer):
        return pltpu.make_async_remote_copy(
            src_ref=src,
            dst_ref=dst,
            send_sem=send_sem,
            recv_sem=recv_sem,
            device_id={axis: peer},
            device_id_type=pl.DeviceIdType.MESH,
        )

    def one_hot(row, first, extent):
        node = lax.broadcasted_iota(jnp.int32, (extent, face), 0) + first
        if row == 0:
            node = node + (count - 1) * nodes
        return jnp.where(face_ref[0, row : row + 1, :] == node, 1.0, 0.0).astype(F32)

    def mask(c):
        return live[c].astype(BF16)

    def relayout(chunk):
        at = slice(chunk * face, (chunk + 1) * face)
        wide = res_in[at].astype(F32).reshape(face * cells, res)
        for h in range(res // 128):
            lanes = slice(h * 128, (h + 1) * 128)
            res_wide[h] = wide[:, lanes]
            for c in range(cells):
                res_ref[c, at, lanes] = res_wide[h, pl.ds(c, face, stride=cells), :].astype(BF16)

    chunks = nodes // face

    def first_chunks():
        load.wait()
        for chunk in range(chunks // 2):
            relayout(chunk)

    def last_chunks():
        for chunk in range(chunks // 2, chunks):
            relayout(chunk)

    def rows_of(c):
        return slice(c * width, (c + 1) * width)

    def face_copy(step, b, way):
        return remote(
            face_out.at[step, b, way],
            face_in.at[step, b, way],
            face_send_sem.at[step, b, way],
            face_recv_sem.at[step, b, way],
            "dom",
            d + 1 if way == RIGHT else d - 1,
        )

    def apply_operator(step, b, field, meanwhile=None):
        local[...] = dot_nn(field(None), stiff_ref[...])
        last_tail = jnp.zeros((width, nodes - window), F32)
        for c in range(cells):
            value = scale[c] * local[rows_of(c), :] + pot_ref[c : c + 1, :] * field(
                c
            ).astype(F32)
            local[rows_of(c), :] = value
            last_tail = last_tail + last[c] * value[:, window:]
        face_out[step, b, RIGHT] = dot_nn(
            last_tail, one_hot(0, window, nodes - window), lax.Precision.HIGHEST
        )
        face_out[step, b, LEFT] = dot_nn(
            local[rows_of(0), :face], one_hot(1, 0, face), lax.Precision.HIGHEST
        )
        for way, there in ((RIGHT, has_next), (LEFT, has_prev)):

            @pl.when(there)
            def _():
                face_copy(step, b, way).start()

            pending.append((there, partial(face_copy, step, b, way)))
        for c in range(cells - 1):
            pair = live[c + 1]
            tail = local[rows_of(c), window:]
            head = local[rows_of(c + 1), :face]
            padded = head
            if offset:
                padded = jnp.concatenate([jnp.zeros((width, offset), F32), head], axis=1)
            local[rows_of(c), window:] = tail + pair * padded
            local[rows_of(c + 1), :face] = head + pair * tail[:, offset:]
        if meanwhile is not None:
            meanwhile()
        for way, source in ((RIGHT, has_prev), (LEFT, has_next)):

            @pl.when(source)
            def _():
                face_copy(step, b, way).wait_recv()

            @pl.when(jnp.logical_not(source))
            def _():
                face_in[step, b, way] = jnp.zeros((width, face), F32)

        local[rows_of(0), :face] += dot_nt(
            face_in[step, b, RIGHT], one_hot(1, 0, face), lax.Precision.HIGHEST
        )
        tail_add = dot_nt(
            face_in[step, b, LEFT], one_hot(0, window, nodes - window), lax.Precision.HIGHEST
        )
        for c in range(cells):
            local[rows_of(c), window:] += last[c] * tail_add

    def filter_block(b, one=None, two=None):
        def first(c):
            if c is None:
                parts = [first(i) for i in range(cells)]
                return jnp.concatenate(parts, axis=0)
            return start_ref[b, c] * mask(c)

        def second(c):
            return inner[...] if c is None else inner[rows_of(c), :]

        apply_operator(0, b, first, one)
        for c in range(cells):
            value = live[c] * local[rows_of(c), :]
            inner[rows_of(c), :] = ((value - CENTER * first(c).astype(F32)) / HALF_WIDTH).astype(
                BF16
            )
        apply_operator(1, b, second, two)
        for c in range(cells):
            value = live[c] * local[rows_of(c), :]
            states[b, c, own, :] = (
                2.0 * (value - CENTER * second(c).astype(F32)) / HALF_WIDTH - first(c).astype(F32)
            ).astype(BF16)

    def gather_copy(b, way, shard):
        at = states.at[b, :, pl.ds(pl.multiple_of(shard * width, width), width), :]
        return remote(
            at,
            at,
            gather_send_sem.at[b, way, shard],
            gather_recv_sem.at[b, shard],
            "st",
            s + 1 if way == RIGHT else s - 1,
        )

    def gather_send(b, way, shard, there):
        @pl.when(there)
        def _():
            gather_copy(b, way, shard).start()

        pending.append((there, partial(gather_copy, b, way, shard)))

    def gather_start(b, k):
        gather_send(b, RIGHT, s, both(has_right, s == k))
        gather_send(b, LEFT, s, both(has_left, s + k == sts - 1))

    def gather_steps(b):
        for k in range(1, sts):
            for way, shard, here, more in (
                (RIGHT, s - k, s >= k, has_right),
                (LEFT, s + k, s + k < sts, has_left),
            ):

                @pl.when(here)
                def _():
                    gather_copy(b, way, shard).wait_recv()

                gather_send(b, way, shard, both(here, more))
            if b + 1 < blocks:
                gather_start(b + 1, k)

    def contract(b):
        part[b] = jnp.zeros(part.shape[1:], F32)

        def add_cell(c, carry):
            block = states[b, c]
            found = dot_nn(block, res_ref[c])
            for h in range(res // total_states):
                at = slice(h * total_states, (h + 1) * total_states)
                part[b, at, :] += found[:, at]
            part[b, res : res + total_states, :] += dot_nt(block, block)
            return carry

        lax.fori_loop(0, cells, add_cell, 0)

    def slice_of(peer):
        return pl.ds(pl.multiple_of(peer * rows, 8), rows)

    def one_copy(b, k):
        peer = dom_peer(k)
        return remote(
            part.at[b, slice_of(peer)],
            part_recv.at[b, k],
            one_send_sem.at[b, k],
            one_recv_sem.at[b, k],
            "dom",
            peer,
        )

    def two_copy(b, k):
        at = total.at[b, slice_of(d)]
        return remote(
            at, at, two_send_sem.at[b, k], two_recv_sem.at[b, k], "dom", dom_peer(k)
        )

    def from_peer(b, k):
        at = total.at[b, slice_of(dom_peer(doms - k))]
        return remote(
            at, at, two_send_sem.at[b, k], two_recv_sem.at[b, k], "dom", dom_peer(doms - k)
        )

    def all_reduce(b):
        def loop(body):
            def step(k, carry):
                body(k)
                return carry

            lax.fori_loop(1, doms, step, 0)

        loop(lambda k: one_copy(b, k).start())
        total[b, slice_of(d), :] = part[b, slice_of(d), :]

        def add(k):
            one_copy(b, k).wait_recv()
            total[b, slice_of(d), :] += part_recv[b, k]

        loop(add)
        loop(lambda k: two_copy(b, k).start())
        loop(lambda k: from_peer(b, k).wait_recv())

    def finish_reduce(b):
        def step(k, carry):
            one_copy(b, k).wait_send()
            two_copy(b, k).wait_send()
            return carry

        lax.fori_loop(1, doms, step, 0)

    def coefficients(b):
        gram = total[b, res : res + total_states, :]
        shape = (total_states, total_states)
        eye = (
            lax.broadcasted_iota(jnp.int32, shape, 0) == lax.broadcasted_iota(jnp.int32, shape, 1)
        ).astype(F32)
        along = jnp.sum(gram * eye, axis=0, keepdims=True) / total_nodes + EPSILON
        down = jnp.sum(gram * eye, axis=1, keepdims=True) / total_nodes + EPSILON
        root_i, root_j = lax.rsqrt(along), lax.rsqrt(down)
        mixing = root_i * (1.5 * eye - 0.5 * (gram * root_i * root_j / total_nodes))
        mix[b] = mixing.astype(BF16)
        for h in range(res // total_states):
            at = slice(h * total_states, (h + 1) * total_states)
            proj[b, :, at] = dot_nn(mixing, total[b, at, :], lax.Precision.HIGHEST).astype(BF16)

    def to(way):
        return s + 1 if way == RIGHT else s - 1

    origin = {RIGHT: s == 0, LEFT: s == sts - 1}
    sends = {RIGHT: has_right, LEFT: has_left}
    receives = {RIGHT: has_left, LEFT: has_right}
    near_end = {RIGHT: s == 1, LEFT: s == sts - 2}
    pieces = ((0, moved), (moved, cells))

    def near_copy(way, c):
        return remote(
            res_ref.at[c],
            res_near.at[way, c],
            near_send_sem.at[way, c],
            near_recv_sem.at[way, c],
            "st",
            to(way),
        )

    def near_start(c):
        for way in (RIGHT, LEFT):
            there = both(origin[way], sends[way])

            @pl.when(there)
            def _():
                near_copy(way, c).start()

            pending.append((there, partial(near_copy, way, c)))

    def near_wait():
        for way in (RIGHT, LEFT):

            @pl.when(near_end[way])
            def _():
                for c in range(moved):
                    near_copy(way, c).wait_recv()

    def coef_copy(b, way):
        return remote(
            proj.at[b],
            proj_near.at[way, b],
            coef_send_sem.at[way, b],
            coef_recv_sem.at[way, b],
            "st",
            to(way),
        )

    def coef_start(b):
        for way in (RIGHT, LEFT):
            there = both(origin[way], sends[way])

            @pl.when(there)
            def _():
                coef_copy(b, way).start()

            pending.append((there, partial(coef_copy, b, way)))

    def share_copy(b, t, way, piece):
        at = pl.ds(pieces[piece][0], pieces[piece][1] - pieces[piece][0])
        return remote(
            share.at[b, t, at],
            share_recv.at[way, b, t, at],
            share_send_sem.at[b, t, piece],
            share_recv_sem.at[way, b, t, piece],
            "st",
            to(way),
        )

    def targets():
        for j in range(sts - 1):
            far = sts - 1 - j
            yield far, RIGHT, far > s
            yield j, LEFT, j < s

    def share_start(b):
        def one(c, carry):
            found = dot_nt(proj[b], res_ref[c])
            for t in range(sts):
                share[b, t, c] = found[t * width : (t + 1) * width, :].astype(BF16)

                @pl.when(t == s)
                def _():
                    retained[b, c] = -found[t * width : (t + 1) * width, :]

            return carry

        lax.fori_loop(0, cells, one, 0)
        for t, way, ahead in targets():

            @pl.when(both(ahead, origin[way]))
            def _():
                share_copy(b, t, way, 1).start()

            for piece in (0, 1):
                there = ahead if piece else both(ahead, jnp.logical_not(origin[way]))
                pending.append((there, partial(share_copy, b, t, way, piece)))

    def retain(b):
        def one(c, carry):
            retained[b, c] += dot_nn(mix[b, own, :], states[b, c])
            return carry

        lax.fori_loop(0, cells, one, 0)

    def near_share(b):
        for way in (RIGHT, LEFT):

            @pl.when(near_end[way])
            def _():
                coef_copy(b, way).wait_recv()
                for c in range(moved):
                    found = dot_nt(proj_near[way, b], res_near[way, c])
                    for t in range(sts):
                        passed = t > s if way == RIGHT else t < s

                        @pl.when(passed)
                        def _():
                            share[b, t, c] = (
                                share[b, t, c].astype(F32)
                                + found[t * width : (t + 1) * width, :]
                            ).astype(BF16)

                        @pl.when(t == s)
                        def _():
                            retained[b, c] -= found[t * width : (t + 1) * width, :]

    def share_forward(b, piece):
        for t, way, ahead in targets():

            @pl.when(both(ahead, jnp.logical_not(origin[way])))
            def _():
                def absorb():
                    share_copy(b, t, way, piece).wait_recv()

                    def one(c, carry):
                        share[b, t, c] = (
                            share[b, t, c].astype(F32) + share_recv[way, b, t, c].astype(F32)
                        ).astype(BF16)
                        return carry

                    lax.fori_loop(*pieces[piece], one, 0)

                if piece:
                    absorb()
                else:
                    pl.when(jnp.logical_not(near_end[way]))(absorb)
                share_copy(b, t, way, piece).start()

    def finish(b):
        for piece in (0, 1):
            for way in (RIGHT, LEFT):
                source = receives[way]
                if piece == 0:
                    source = both(source, jnp.logical_not(near_end[way]))

                @pl.when(source)
                def _():
                    share_copy(b, s, way, piece).wait_recv()

                    def one(c, carry):
                        retained[b, c] -= share_recv[way, b, s, c].astype(F32)
                        return carry

                    lax.fori_loop(*pieces[piece], one, 0)

            for c in range(*pieces[piece]):
                out_ref[b, c] = retained[b, c].astype(BF16) * mask(c)

    filter_block(0, first_chunks, last_chunks)
    for k in range(sts):
        gather_start(0, k)
    near_start(0)
    for b in range(1, blocks):
        filter_block(b)
    if blocks > 1:
        gather_start(1, 0)
    for c in range(1, moved):
        near_start(c)
    gather_steps(0)
    for b in range(blocks):
        contract(b)
        all_reduce(b)
        if b:
            share_forward(b - 1, 1)
        coefficients(b)
        coef_start(b)
        share_start(b)
        if b + 1 < blocks:
            gather_steps(b + 1)
        if b == 0:
            near_wait()
        near_share(b)
        share_forward(b, 0)
        retain(b)
        if b:
            finish(b - 1)
    share_forward(blocks - 1, 1)
    finish(blocks - 1)
    for there, make in pending:

        @pl.when(there)
        def _():
            make().wait_send()

    for b in range(blocks):
        finish_reduce(b)


def on_device(start_block, resident, stiffness, cell_scale, potential, cell_count, face_index):
    blocks, cells, width, nodes = start_block.shape
    res = resident.shape[0]
    face = face_index.shape[2]
    doms, sts = lax.axis_size("dom"), lax.axis_size("st")
    total_states = sts * width
    rows = -(-(res + total_states) // (8 * doms)) * 8
    moved = 3 * cells // 8
    sizes = (doms, sts, blocks, cells, width, nodes, face, res, rows, moved)
    dma = pltpu.SemaphoreType.DMA
    vmem = pl.BlockSpec(memory_space=pltpu.VMEM)
    smem = pl.BlockSpec(memory_space=pltpu.SMEM)
    return pl.pallas_call(
        partial(kernel, sizes),
        out_shape=jax.ShapeDtypeStruct((blocks, cells, width, nodes), BF16),
        in_specs=[smem, smem, vmem, pl.BlockSpec(memory_space=pl.ANY), vmem, vmem, vmem],
        out_specs=vmem,
        scratch_shapes=[
            pltpu.VMEM((cells * width, nodes), F32),
            pltpu.VMEM((cells * width, nodes), BF16),
            pltpu.VMEM((blocks, cells, total_states, nodes), BF16),
            pltpu.VMEM((blocks, doms * rows, total_states), F32),
            pltpu.VMEM((blocks, doms, rows, total_states), F32),
            pltpu.VMEM((blocks, doms * rows, total_states), F32),
            pltpu.VMEM((blocks, total_states, total_states), BF16),
            pltpu.VMEM((blocks, total_states, res), BF16),
            pltpu.VMEM((blocks, sts, cells, width, nodes), BF16),
            pltpu.VMEM((2, blocks, sts, cells, width, nodes), BF16),
            pltpu.VMEM((nodes, cells, res), BF16),
            pltpu.VMEM((res // 128, face * cells, 128), F32),
            pltpu.VMEM((cells, nodes, res), BF16),
            pltpu.VMEM((2, moved, nodes, res), BF16),
            pltpu.VMEM((2, blocks, total_states, res), BF16),
            pltpu.VMEM((blocks, cells, width, nodes), F32),
            pltpu.VMEM((2, blocks, 2, width, face), F32),
            pltpu.VMEM((2, blocks, 2, width, face), F32),
            dma((2, blocks, 2)),
            dma((2, blocks, 2)),
            dma((blocks, 2, sts)),
            dma((blocks, sts)),
            dma((blocks, doms)),
            dma((blocks, doms)),
            dma((blocks, doms)),
            dma((blocks, doms)),
            dma((blocks, sts, 2)),
            dma((2, blocks, sts, 2)),
            dma,
            dma((2, moved)),
            dma((2, moved)),
            dma((2, blocks)),
            dma((2, blocks)),
        ],
        compiler_params=pltpu.CompilerParams(
            collective_id=0, has_side_effects=True, vmem_limit_bytes=60 * 1024 * 1024
        ),
    )(
        cell_scale,
        cell_count,
        start_block,
        jnp.transpose(resident, (2, 1, 0)),
        stiffness,
        potential,
        face_index,
    )


def solution(mesh):
    return jax.shard_map(
        on_device,
        mesh=mesh,
        in_specs=(
            P(None, "dom", "st", None),
            P("st", "dom", None),
            P(),
            P("dom"),
            P("dom", None),
            P("dom"),
            P("dom", None, None),
        ),
        out_specs=P(None, "dom", "st", None),
        check_vma=False,
    )
```

profile of v0, /device:TPU:0, one launch (start us, length us, event | category | flops | bytes accessed | tf_op | source)
XLA Modules:
  0.0 135.9 jit_solution(10770305501972007058)
XLA Ops:
  0.7 133.2 %shard_map.73 = bf16[2,8,32,729]{3,2,1,0:T(8,128)(2,1)} custom-call(f32[8]{0:T(128)} %scale_ref.1, s32[1]{0:T(128)S(6)} %copy.9.count_ref, bf16[2,8,32,729]{3,2,1,0:T(8,128)(2,1)} %start_ref.1, bf16[729,8,256]{2,1,0:T(8,128)(2,1)} %bitcast.1, bf16[729,729]{1,0:T(8,128)(2,1)} %stiff_ref.1, f32[8,729]{1,0:T(8,128)} %pot_ref.1, s32[1,2,81]{2,1,0:T(2,128)} %face_ref.1), custom_call_target="tpu_custom_call" | custom-call | tf_op jit(solution)/shard_map/pallas_call | solution.py:587
  133.8 2.1 %copy.10 = bf16[2,8,32,729]{3,2,1,0:T(8,128)(2,1)} copy(bf16[2,8,32,729]{3,2,1,0:T(8,128)(2,1)} %shard_map.73) | data formatting | bytes 1492992
where the time goes:
time: 136 us
  Pallas kernels  133 us (98%)
  local copies, waits for them, and re-layouts  2.06 us (2%)
    pallas_call x1, Pallas kernels, on_device(): pl.pallas_call(partial(kernel, sizes), out_shape=jax.ShapeDtypeStruct((bl...  133 us

commit v1 on v0

v1 whole, which is shorter than its diff:
```python
from functools import partial

import jax
import jax.numpy as jnp
from jax import lax
from jax.experimental import pallas as pl
from jax.experimental.pallas import tpu as pltpu
from jax.sharding import PartitionSpec as P

CENTER = 0.5
HALF_WIDTH = 2.0
EPSILON = 1e-06
F32 = jnp.float32
BF16 = jnp.bfloat16
WIRE = BF16
RIGHT, LEFT = 0, 1
MESH = pl.DeviceIdType.MESH


def dot_nn(a, b, precision=None):
    return lax.dot_general(
        a, b, (((1,), (0,)), ((), ())), precision=precision, preferred_element_type=F32
    )


def dot_nt(a, b, precision=None):
    return lax.dot_general(
        a, b, (((1,), (1,)), ((), ())), precision=precision, preferred_element_type=F32
    )


def both(*conditions):
    found = conditions[0]
    for condition in conditions[1:]:
        found = jnp.logical_and(found, condition)
    return found


def kernel(
    sizes,
    scale_ref,
    count_ref,
    start_ref,
    res_hbm,
    stiff_ref,
    pot_ref,
    face_ref,
    out_ref,
    local,
    inner,
    states,
    part,
    wire,
    part_recv,
    total,
    mix,
    proj,
    share,
    share_recv,
    res_in,
    res_wide,
    res_ref,
    res_near,
    proj_near,
    retained,
    face_out,
    face_in,
    face_send_sem,
    face_recv_sem,
    gather_send_sem,
    gather_recv_sem,
    one_send_sem,
    one_recv_sem,
    two_send_sem,
    two_recv_sem,
    share_send_sem,
    share_recv_sem,
    load_sem,
    near_send_sem,
    near_recv_sem,
    coef_send_sem,
    coef_recv_sem,
):
    doms, sts, blocks, cells, width, nodes, face, res, rows, moved = sizes
    total_states = sts * width
    total_nodes = float(doms * cells * nodes)
    window = (nodes - face) // 128 * 128
    offset = nodes - face - window
    d = lax.axis_index("dom")
    s = lax.axis_index("st")
    has_right, has_left = s < sts - 1, s > 0
    has_next, has_prev = d < doms - 1, d > 0
    own = pl.ds(pl.multiple_of(s * width, width), width)
    steps = sts - 1
    last_step = jnp.maximum(s, steps - s)
    pending = []
    count = count_ref[0]
    scale = [scale_ref[c] for c in range(cells)]
    live = [jnp.where(c < count, 1.0, 0.0).astype(F32) for c in range(cells)]
    last = [jnp.where(c == count - 1, 1.0, 0.0).astype(F32) for c in range(cells)]
    load = pltpu.make_async_copy(res_hbm, res_in, load_sem)
    load.start()

    origin = {RIGHT: s == 0, LEFT: s == steps}
    sends = {RIGHT: has_right, LEFT: has_left}
    receives = {RIGHT: has_left, LEFT: has_right}
    near_end = {RIGHT: s == 1, LEFT: s == steps - 1}

    def to(way):
        return s + 1 if way == RIGHT else s - 1

    def dom_peer(k):
        return lax.rem(d + k, doms)

    barrier = pltpu.get_barrier_semaphore()

    def greet(k, carry):
        pl.semaphore_signal(barrier, inc=1, device_id={"dom": dom_peer(k)}, device_id_type=MESH)
        return carry

    lax.fori_loop(1, doms, greet, 0)
    for way in (RIGHT, LEFT):

        @pl.when(sends[way])
        def _():
            pl.semaphore_signal(barrier, inc=1, device_id={"st": to(way)}, device_id_type=MESH)

    neighbours = has_right.astype(jnp.int32) + has_left.astype(jnp.int32)
    pl.semaphore_wait(barrier, doms - 1 + neighbours)

    def remote(src, dst, send_sem, recv_sem, axis, peer):
        return pltpu.make_async_remote_copy(
            src_ref=src,
            dst_ref=dst,
            send_sem=send_sem,
            recv_sem=recv_sem,
            device_id={axis: peer},
            device_id_type=MESH,
        )

    def one_hot(row, first, extent):
        node = lax.broadcasted_iota(jnp.int32, (extent, face), 0) + first
        if row == 0:
            node = node + (count - 1) * nodes
        return jnp.where(face_ref[0, row : row + 1, :] == node, 1.0, 0.0).astype(F32)

    def mask(c):
        return live[c].astype(BF16)

    def relayout():
        load.wait()
        for chunk in range(nodes // face):
            at = slice(chunk * face, (chunk + 1) * face)
            wide = res_in[at].astype(F32).reshape(face * cells, res)
            for h in range(res // 128):
                lanes = slice(h * 128, (h + 1) * 128)
                res_wide[h] = wide[:, lanes]
                for c in range(cells):
                    res_ref[c, at, lanes] = res_wide[h, pl.ds(c, face, stride=cells), :].astype(BF16)


    def rows_of(c):
        return slice(c * width, (c + 1) * width)

    def face_copy(step, b, way):
        return remote(
            face_out.at[step, b, way],
            face_in.at[step, b, way],
            face_send_sem.at[step, b, way],
            face_recv_sem.at[step, b, way],
            "dom",
            d + 1 if way == RIGHT else d - 1,
        )

    def first(b, c):
        if c is None:
            return jnp.concatenate([first(b, i) for i in range(cells)], axis=0)
        return start_ref[b, c] * mask(c)

    def second(b, c):
        return inner[b] if c is None else inner[b, rows_of(c), :]

    def operator_begin(step, b):
        field = partial(second if step else first, b)
        local[b] = dot_nn(field(None), stiff_ref[...])
        last_tail = jnp.zeros((width, nodes - window), F32)
        for c in range(cells):
            value = scale[c] * local[b, rows_of(c), :] + pot_ref[c : c + 1, :] * field(c).astype(F32)
            local[b, rows_of(c), :] = value
            last_tail = last_tail + last[c] * value[:, window:]
        face_out[step, b, RIGHT] = dot_nn(
            last_tail, one_hot(0, window, nodes - window), lax.Precision.HIGHEST
        )
        face_out[step, b, LEFT] = dot_nn(
            local[b, rows_of(0), :face], one_hot(1, 0, face), lax.Precision.HIGHEST
        )
        for way, there in ((RIGHT, has_next), (LEFT, has_prev)):

            @pl.when(there)
            def _():
                face_copy(step, b, way).start()

            pending.append((there, partial(face_copy, step, b, way)))
        for c in range(cells - 1):
            pair = live[c + 1]
            tail = local[b, rows_of(c), window:]
            head = local[b, rows_of(c + 1), :face]
            padded = head
            if offset:
                padded = jnp.concatenate([jnp.zeros((width, offset), F32), head], axis=1)
            local[b, rows_of(c), window:] = tail + pair * padded
            local[b, rows_of(c + 1), :face] = head + pair * tail[:, offset:]

    def operator_end(step, b):
        for way, source in ((RIGHT, has_prev), (LEFT, has_next)):

            @pl.when(source)
            def _():
                face_copy(step, b, way).wait_recv()

            @pl.when(jnp.logical_not(source))
            def _():
                face_in[step, b, way] = jnp.zeros((width, face), F32)

        local[b, rows_of(0), :face] += dot_nt(
            face_in[step, b, RIGHT], one_hot(1, 0, face), lax.Precision.HIGHEST
        )
        tail_add = dot_nt(
            face_in[step, b, LEFT], one_hot(0, window, nodes - window), lax.Precision.HIGHEST
        )
        for c in range(cells):
            local[b, rows_of(c), window:] += last[c] * tail_add
        for c in range(cells):
            value = live[c] * local[b, rows_of(c), :]
            if step == 0:
                inner[b, rows_of(c), :] = (
                    (value - CENTER * first(b, c).astype(F32)) / HALF_WIDTH
                ).astype(BF16)
            else:
                states[b, c, own, :] = (
                    2.0 * (value - CENTER * second(b, c).astype(F32)) / HALF_WIDTH
                    - first(b, c).astype(F32)
                ).astype(BF16)


    def of_shard(shard):
        return pl.ds(pl.multiple_of(shard * width, width), width)

    def gather_copy(b, way, shard, c):
        at = states.at[b, c, of_shard(shard), :]
        return remote(
            at, at, gather_send_sem.at[b, way, shard], gather_recv_sem.at[b, shard, c], "st", to(way)
        )

    def gather_whole(b, way, shard):
        at = states.at[b, :, of_shard(shard), :]
        return remote(
            at, at, gather_send_sem.at[b, way, shard], gather_recv_sem.at[b, shard, 0], "st", to(way)
        )

    def gather_own(b, way, there):
        @pl.when(both(there, sends[way]))
        def _():
            def one(c, carry):
                gather_copy(b, way, s, c).start()
                return carry

            lax.fori_loop(0, cells, one, 0)

    def gather_start(b, k):
        gather_own(b, RIGHT, s == k)
        gather_own(b, LEFT, s + k == steps)

    def gather_flat(b, begin, end):
        def one(i, carry):
            k = lax.div(i, cells) + 1
            c = lax.rem(i, cells)
            for way, shard, here in ((LEFT, s + k, s + k < sts), (RIGHT, s - k, s >= k)):

                @pl.when(here)
                def _():
                    gather_copy(b, way, shard, c).wait_recv()

                    @pl.when(sends[way])
                    def _():
                        gather_copy(b, way, shard, c).start()

            @pl.when(k == last_step)
            def _():
                contract(b, c)

            if b + 1 < blocks:

                @pl.when(c == cells - 1)
                def _():
                    gather_start(b + 1, k)

            return carry

        lax.fori_loop(begin, end, one, 0)

    def gather_drain(b):
        def one(shard, carry):
            for way, passed in ((RIGHT, shard <= s), (LEFT, shard >= s)):

                @pl.when(both(passed, sends[way]))
                def _():
                    gather_whole(b, way, shard).wait_send()

            return carry

        lax.fori_loop(0, sts, one, 0)


    def contract(b, c):
        block = states[b, c]
        found = dot_nn(block, res_ref[c])
        for h in range(res // total_states):
            at = slice(h * total_states, (h + 1) * total_states)
            part[b, at, :] += found[:, at]
        part[b, res : res + total_states, :] += dot_nt(block, block)

    def slice_of(peer):
        return pl.ds(pl.multiple_of(peer * rows, 16), rows)

    def one_copy(b, k):
        peer = dom_peer(k)
        return remote(
            wire.at[b, slice_of(peer)],
            part_recv.at[b, k],
            one_send_sem.at[b, k],
            one_recv_sem.at[b, k],
            "dom",
            peer,
        )

    def two_copy(b, k):
        at = total.at[b, slice_of(d)]
        return remote(at, at, two_send_sem.at[b, k], two_recv_sem.at[b, k], "dom", dom_peer(k))

    def from_peer(b, k):
        peer = dom_peer(doms - k)
        at = total.at[b, slice_of(peer)]
        return remote(at, at, two_send_sem.at[b, k], two_recv_sem.at[b, k], "dom", peer)

    def peers(body):
        def step(k, carry):
            body(k)
            return carry

        lax.fori_loop(1, doms, step, 0)

    def reduce_start(b):
        wire[b] = part[b].astype(WIRE)
        peers(lambda k: one_copy(b, k).start())

    def reduce_middle(b):
        def add(k, found):
            one_copy(b, k).wait_recv()
            return found + part_recv[b, k].astype(F32)

        found = lax.fori_loop(1, doms, add, part[b, slice_of(d), :])
        total[b, slice_of(d), :] = found.astype(WIRE)
        peers(lambda k: two_copy(b, k).start())

    def reduce_end(b):
        peers(lambda k: from_peer(b, k).wait_recv())

    def reduce_drain(b):
        def one(k):
            one_copy(b, k).wait_send()
            two_copy(b, k).wait_send()

        peers(one)

    def coefficients(b):
        gram = total[b, res : res + total_states, :].astype(F32)
        shape = (total_states, total_states)
        eye = (
            lax.broadcasted_iota(jnp.int32, shape, 0) == lax.broadcasted_iota(jnp.int32, shape, 1)
        ).astype(F32)
        along = jnp.sum(gram * eye, axis=0, keepdims=True) / total_nodes + EPSILON
        down = jnp.sum(gram * eye, axis=1, keepdims=True) / total_nodes + EPSILON
        root_i, root_j = lax.rsqrt(along), lax.rsqrt(down)
        mixing = root_i * (1.5 * eye - 0.5 * (gram * root_i * root_j / total_nodes))
        mix[b] = mixing.astype(BF16)
        for h in range(res // total_states):
            at = slice(h * total_states, (h + 1) * total_states)
            proj[b, :, at] = dot_nn(
                mixing, total[b, at, :].astype(F32), lax.Precision.HIGHEST
            ).astype(BF16)


    def near_copy(way, c):
        return remote(
            res_ref.at[c],
            res_near.at[way, c],
            near_send_sem.at[way, c],
            near_recv_sem.at[way, c],
            "st",
            to(way),
        )

    def near_start(c):
        if c >= moved:
            return
        for way in (RIGHT, LEFT):
            there = both(origin[way], sends[way])

            @pl.when(there)
            def _():
                near_copy(way, c).start()

            pending.append((there, partial(near_copy, way, c)))

    def coef_copy(b, way):
        return remote(
            proj.at[b],
            proj_near.at[way, b],
            coef_send_sem.at[way, b],
            coef_recv_sem.at[way, b],
            "st",
            to(way),
        )

    def coef_start(b):
        if not moved:
            return
        for way in (RIGHT, LEFT):
            there = both(origin[way], sends[way])

            @pl.when(there)
            def _():
                coef_copy(b, way).start()

            pending.append((there, partial(coef_copy, b, way)))


    def share_copy(b, t, way, c):
        return remote(
            share.at[b, t, c],
            share_recv.at[way, b, t, c],
            share_send_sem.at[b, t],
            share_recv_sem.at[way, b, t, c],
            "st",
            to(way),
        )

    def share_whole(b, t, way, begin):
        at = pl.ds(begin, cells - begin)
        return remote(
            share.at[b, t, at],
            share_recv.at[way, b, t, at],
            share_send_sem.at[b, t],
            share_recv_sem.at[way, b, t, 0],
            "st",
            to(way),
        )

    def ahead(way):
        if way == RIGHT:
            return steps - s, lambda i: steps - i
        return s, lambda i: i

    def share_start(b):
        def one(c, carry):
            found = dot_nt(proj[b], res_ref[c])
            for t in range(sts):
                piece = found[t * width : (t + 1) * width, :]
                share[b, t, c] = piece.astype(BF16)

                @pl.when(t == s)
                def _():
                    retained[b, c] = -piece

            for way in (RIGHT, LEFT):

                @pl.when(both(origin[way], c >= moved))
                def _():
                    number, target = ahead(way)

                    def send(i, carry):
                        share_copy(b, target(i), way, c).start()
                        return carry

                    lax.fori_loop(0, number, send, 0)

            return carry

        lax.fori_loop(0, cells, one, 0)

    def share_drain(b):
        def one(t, carry):
            for way, passed in ((RIGHT, t > s), (LEFT, t < s)):

                @pl.when(both(passed, origin[way]))
                def _():
                    share_whole(b, t, way, moved).wait_send()

                @pl.when(both(passed, jnp.logical_not(origin[way])))
                def _():
                    share_whole(b, t, way, 0).wait_send()

            return carry

        lax.fori_loop(0, sts, one, 0)

    def retain(b):
        def one(c, carry):
            retained[b, c] += dot_nn(mix[b, own, :], states[b, c])
            return carry

        lax.fori_loop(0, cells, one, 0)

    def absorb(b, way, c):
        number, target = ahead(way)

        def one(i, carry):
            t = target(i)
            share_copy(b, t, way, c).wait_recv()
            share[b, t, c] = (
                share[b, t, c].astype(F32) + share_recv[way, b, t, c].astype(F32)
            ).astype(BF16)
            share_copy(b, t, way, c).start()
            return carry

        lax.fori_loop(0, number, one, 0)
        share_copy(b, s, way, c).wait_recv()
        retained[b, c] -= share_recv[way, b, s, c].astype(F32)

    def absorb_near(b, way, c):
        if b == 0:
            near_copy(way, c).wait_recv()

        @pl.when(c == 0)
        def _():
            coef_copy(b, way).wait_recv()

        found = dot_nt(proj_near[way, b], res_near[way, c])
        for t in reversed(range(sts)) if way == RIGHT else range(sts):
            piece = found[t * width : (t + 1) * width, :]

            @pl.when(t > s if way == RIGHT else t < s)
            def _():
                share[b, t, c] = (share[b, t, c].astype(F32) + piece).astype(BF16)
                share_copy(b, t, way, c).start()

            @pl.when(t == s)
            def _():
                retained[b, c] -= piece

    def chain(b, begin, end):
        def one(j, carry):
            for way, lag in ((RIGHT, s), (LEFT, steps - s)):
                c = j - lag
                here = both(receives[way], c >= 0, c < cells)
                near = both(near_end[way], c < moved)
                if moved:

                    @pl.when(both(here, near))
                    def _():
                        absorb_near(b, way, c)

                @pl.when(both(here, jnp.logical_not(near)))
                def _():
                    absorb(b, way, c)

            c = j - last_step

            @pl.when(both(c >= 0, c < cells))
            def _():
                alive = jnp.where(c < count, 1.0, 0.0).astype(BF16)
                out_ref[b, c] = retained[b, c].astype(BF16) * alive

            return carry

        lax.fori_loop(begin, end, one, 0)


    for b in range(blocks):
        part[b] = jnp.zeros(part.shape[1:], F32)
    for b in range(blocks):
        operator_begin(0, b)
        if b == 0:
            relayout()
            near_start(0)
    for b in range(blocks):
        operator_end(0, b)
        operator_begin(1, b)
    for b in range(blocks):
        operator_end(1, b)
        if b == 0:
            for k in range(sts):
                gather_start(0, k)
            near_start(1)
        if b == 1:
            gather_start(1, 0)
    for c in range(2, moved):
        near_start(c)

    half = cells // 2
    whole = steps * cells
    links = cells + steps
    cut_one, cut_two = links // 3 + 2, links // 3 + 5
    gather_flat(0, 0, whole)
    reduce_start(0)
    for b in range(blocks):
        following, previous = b + 1 < blocks, b > 0
        if following:
            gather_flat(b + 1, 0, half)
        if previous:
            chain(b - 1, 0, cut_one)
        reduce_middle(b)
        if following:
            gather_flat(b + 1, half, cells)
        if previous:
            chain(b - 1, cut_one, cut_two)
        reduce_end(b)
        coefficients(b)
        coef_start(b)
        share_start(b)
        if previous:
            chain(b - 1, cut_two, links)
        retain(b)
        if following:
            gather_flat(b + 1, cells, whole)
            reduce_start(b + 1)
    chain(blocks - 1, 0, links)

    for there, make in pending:

        @pl.when(there)
        def _():
            make().wait_send()

    for b in range(blocks):
        gather_drain(b)
        reduce_drain(b)
        share_drain(b)


def on_device(start_block, resident, stiffness, cell_scale, potential, cell_count, face_index):
    blocks, cells, width, nodes = start_block.shape
    res = resident.shape[0]
    face = face_index.shape[2]
    doms, sts = lax.axis_size("dom"), lax.axis_size("st")
    total_states = sts * width
    rows = -(-(res + total_states) // (16 * doms)) * 16
    moved = 3 * cells // 8 if sts > 3 else 0
    sizes = (doms, sts, blocks, cells, width, nodes, face, res, rows, moved)
    near = max(moved, 1)
    dma = pltpu.SemaphoreType.DMA
    vmem = pl.BlockSpec(memory_space=pltpu.VMEM)
    smem = pl.BlockSpec(memory_space=pltpu.SMEM)
    return pl.pallas_call(
        partial(kernel, sizes),
        out_shape=jax.ShapeDtypeStruct((blocks, cells, width, nodes), BF16),
        in_specs=[smem, smem, vmem, pl.BlockSpec(memory_space=pl.ANY), vmem, vmem, vmem],
        out_specs=vmem,
        scratch_shapes=[
            pltpu.VMEM((blocks, cells * width, nodes), F32),
            pltpu.VMEM((blocks, cells * width, nodes), BF16),
            pltpu.VMEM((blocks, cells, total_states, nodes), BF16),
            pltpu.VMEM((blocks, doms * rows, total_states), F32),
            pltpu.VMEM((blocks, doms * rows, total_states), WIRE),
            pltpu.VMEM((blocks, doms, rows, total_states), WIRE),
            pltpu.VMEM((blocks, doms * rows, total_states), WIRE),
            pltpu.VMEM((blocks, total_states, total_states), BF16),
            pltpu.VMEM((blocks, total_states, res), BF16),
            pltpu.VMEM((blocks, sts, cells, width, nodes), BF16),
            pltpu.VMEM((2, blocks, sts, cells, width, nodes), BF16),
            pltpu.VMEM((nodes, cells, res), BF16),
            pltpu.VMEM((res // 128, face * cells, 128), F32),
            pltpu.VMEM((cells, nodes, res), BF16),
            pltpu.VMEM((2, near, nodes, res), BF16),
            pltpu.VMEM((2, blocks, total_states, res), BF16),
            pltpu.VMEM((blocks, cells, width, nodes), F32),
            pltpu.VMEM((2, blocks, 2, width, face), F32),
            pltpu.VMEM((2, blocks, 2, width, face), F32),
            dma((2, blocks, 2)),
            dma((2, blocks, 2)),
            dma((blocks, 2, sts)),
            dma((blocks, sts, cells)),
            dma((blocks, doms)),
            dma((blocks, doms)),
            dma((blocks, doms)),
            dma((blocks, doms)),
            dma((blocks, sts)),
            dma((2, blocks, sts, cells)),
            dma,
            dma((2, near)),
            dma((2, near)),
            dma((2, blocks)),
            dma((2, blocks)),
        ],
        compiler_params=pltpu.CompilerParams(
            collective_id=0, has_side_effects=True, vmem_limit_bytes=60 * 1024 * 1024
        ),
    )(
        cell_scale,
        cell_count,
        start_block,
        jnp.transpose(resident, (2, 1, 0)),
        stiffness,
        potential,
        face_index,
    )


def solution(mesh):
    return jax.shard_map(
        on_device,
        mesh=mesh,
        in_specs=(
            P(None, "dom", "st", None),
            P("st", "dom", None),
            P(),
            P("dom"),
            P("dom", None),
            P("dom"),
            P("dom", None, None),
        ),
        out_specs=P(None, "dom", "st", None),
        check_vma=False,
    )
```

time: 136 us -> 114 us (0.84)
  Pallas kernels: 133 us -> 111 us
    pallas_call x1, Pallas kernels: 133 us -> 111 us  [on_device(): pl.pallas_call(partial(kernel, sizes), out_shape=jax.ShapeDtypeStruct((bl...]
where the time goes in v1:
time: 114 us
  Pallas kernels  111 us (97%)
  local copies, waits for them, and re-layouts  2.06 us (2%)
    pallas_call x1, Pallas kernels, on_device(): pl.pallas_call(partial(kernel, sizes), out_shape=jax.ShapeDtypeStruct((bl...  111 us

profile of v1, /device:TPU:0, one launch (start us, length us, event | category | flops | bytes accessed | tf_op | source)
XLA Modules:
  0.0 114.0 jit_solution(13402419153164397345)
XLA Ops:
  0.7 111.3 %shard_map.73 = bf16[2,8,32,729]{3,2,1,0:T(8,128)(2,1)} custom-call(f32[8]{0:T(128)} %scale_ref.1, s32[1]{0:T(128)S(6)} %copy.9.count_ref, bf16[2,8,32,729]{3,2,1,0:T(8,128)(2,1)} %start_ref.1, bf16[729,8,256]{2,1,0:T(8,128)(2,1)} %bitcast.1, bf16[729,729]{1,0:T(8,128)(2,1)} %stiff_ref.1, f32[8,729]{1,0:T(8,128)} %pot_ref.1, s32[1,2,81]{2,1,0:T(2,128)} %face_ref.1), custom_call_target="tpu_custom_call" | custom-call | tf_op jit(solution)/shard_map/pallas_call | solution.py:655
  112.0 2.1 %copy.10 = bf16[2,8,32,729]{3,2,1,0:T(8,128)(2,1)} copy(bf16[2,8,32,729]{3,2,1,0:T(8,128)(2,1)} %shard_map.73) | data formatting | bytes 1492992

commit v2 on v1

--- a/solution.py
+++ b/solution.py
@@ -14,6 +14,7 @@
 BF16 = jnp.bfloat16
 WIRE = BF16
 RIGHT, LEFT = 0, 1
+LAG = 3
 MESH = pl.DeviceIdType.MESH
 
 
@@ -40,11 +41,14 @@
     sizes,
     scale_ref,
     count_ref,
-    start_ref,
+    start_hbm,
     res_hbm,
-    stiff_ref,
+    stiff_hbm,
     pot_ref,
     face_ref,
+    out_hbm,
+    start_ref,
+    stiff_ref,
     out_ref,
     local,
     inner,
@@ -76,6 +80,9 @@
     share_send_sem,
     share_recv_sem,
     load_sem,
+    start_sem,
+    stiff_sem,
+    out_sem,
     near_send_sem,
     near_recv_sem,
     coef_send_sem,
@@ -93,15 +100,38 @@
     own = pl.ds(pl.multiple_of(s * width, width), width)
     steps = sts - 1
     last_step = jnp.maximum(s, steps - s)
+    ends = jnp.logical_or(s == 0, s == steps)
     pending = []
     count = count_ref[0]
     scale = [scale_ref[c] for c in range(cells)]
     live = [jnp.where(c < count, 1.0, 0.0).astype(F32) for c in range(cells)]
     last = [jnp.where(c == count - 1, 1.0, 0.0).astype(F32) for c in range(cells)]
-    load = pltpu.make_async_copy(res_hbm, res_in, load_sem)
-    load.start()
+
+    def start_load(b):
+        return pltpu.make_async_copy(start_hbm.at[b], start_ref.at[b], start_sem.at[b])
+
+    def cuts(extent, number):
+        step = -(-extent // (number * 16)) * 16
+        return [pl.ds(at, min(step, extent - at)) for at in range(0, extent, step)]
+
+    def stiff_load(i):
+        at = cuts(nodes, 2)[i]
+        return pltpu.make_async_copy(stiff_hbm.at[at], stiff_ref.at[at], stiff_sem.at[i])
+
+    def res_load(i):
+        at = cuts(nodes, 4)[i]
+        return pltpu.make_async_copy(res_hbm.at[at], res_in.at[at], load_sem.at[i])
+
+    start_load(0).start()
+    for i in range(2):
+        stiff_load(i).start()
+    for b in range(1, blocks):
+        start_load(b).start()
+    for i in range(4):
+        res_load(i).start()
 
     origin = {RIGHT: s == 0, LEFT: s == steps}
+    lag = {RIGHT: LAG * jnp.maximum(s - 1, 0), LEFT: LAG * jnp.maximum(steps - 1 - s, 0)}
     sends = {RIGHT: has_right, LEFT: has_left}
     receives = {RIGHT: has_left, LEFT: has_right}
     near_end = {RIGHT: s == 1, LEFT: s == steps - 1}
@@ -148,7 +178,8 @@
         return live[c].astype(BF16)
 
     def relayout():
-        load.wait()
+        for i in range(4):
+            res_load(i).wait()
         for chunk in range(nodes // face):
             at = slice(chunk * face, (chunk + 1) * face)
             wide = res_in[at].astype(F32).reshape(face * cells, res)
@@ -462,17 +493,23 @@
             return steps - s, lambda i: steps - i
         return s, lambda i: i
 
+    def share_cell(b, c):
+        found = dot_nt(proj[b], res_ref[c])
+        for t in range(sts):
+            piece = found[t * width : (t + 1) * width, :]
+            share[b, t, c] = piece.astype(BF16)
+
+            @pl.when(t == s)
+            def _():
+                retained[b, c] = -piece
+
+    def retain(b, c):
+        retained[b, c] += dot_nn(mix[b, own, :], states[b, c])
+
     def share_start(b):
-        def one(c, carry):
-            found = dot_nt(proj[b], res_ref[c])
-            for t in range(sts):
-                piece = found[t * width : (t + 1) * width, :]
-                share[b, t, c] = piece.astype(BF16)
-
-                @pl.when(t == s)
-                def _():
-                    retained[b, c] = -piece
-
+        def one(i, carry):
+            c = lax.rem(i + moved, cells)
+            share_cell(b, c)
             for way in (RIGHT, LEFT):
 
                 @pl.when(both(origin[way], c >= moved))
@@ -485,9 +522,12 @@
 
                     lax.fori_loop(0, number, send, 0)
 
+            retain(b, c)
             return carry
 
-        lax.fori_loop(0, cells, one, 0)
+        @pl.when(ends)
+        def _():
+            lax.fori_loop(0, cells, one, 0)
 
     def share_drain(b):
         def one(t, carry):
@@ -504,13 +544,6 @@
             return carry
 
         lax.fori_loop(0, sts, one, 0)
-
-    def retain(b):
-        def one(c, carry):
-            retained[b, c] += dot_nn(mix[b, own, :], states[b, c])
-            return carry
-
-        lax.fori_loop(0, cells, one, 0)
 
     def absorb(b, way, c):
         number, target = ahead(way)
@@ -551,8 +584,15 @@
 
     def chain(b, begin, end):
         def one(j, carry):
-            for way, lag in ((RIGHT, s), (LEFT, steps - s)):
-                c = j - lag
+            c = j
+
+            @pl.when(both(jnp.logical_not(ends), c >= 0, c < cells))
+            def _():
+                share_cell(b, c)
+                retain(b, c)
+
+            for way in (RIGHT, LEFT):
+                c = j - lag[way]
                 here = both(receives[way], c >= 0, c < cells)
                 near = both(near_end[way], c < moved)
                 if moved:
@@ -565,12 +605,13 @@
                 def _():
                     absorb(b, way, c)
 
-            c = j - last_step
+            c = j - jnp.maximum(lag[RIGHT], lag[LEFT])
 
             @pl.when(both(c >= 0, c < cells))
             def _():
                 alive = jnp.where(c < count, 1.0, 0.0).astype(BF16)
                 out_ref[b, c] = retained[b, c].astype(BF16) * alive
+                pltpu.make_async_copy(out_ref.at[b, c], out_hbm.at[b, c], out_sem.at[b]).start()
 
             return carry
 
@@ -579,7 +620,12 @@
 
     for b in range(blocks):
         part[b] = jnp.zeros(part.shape[1:], F32)
+    start_load(0).wait()
+    for i in range(2):
+        stiff_load(i).wait()
     for b in range(blocks):
+        if b:
+            start_load(b).wait()
         operator_begin(0, b)
         if b == 0:
             relayout()
@@ -600,8 +646,9 @@
 
     half = cells // 2
     whole = steps * cells
-    links = cells + steps
-    cut_one, cut_two = links // 3 + 2, links // 3 + 5
+    furthest = LAG * max(steps - 1, 0)
+    links = cells + furthest
+    cut_one, cut_two = furthest + 2, furthest + 6
     gather_flat(0, 0, whole)
     reduce_start(0)
     for b in range(blocks):
@@ -621,7 +668,6 @@
         share_start(b)
         if previous:
             chain(b - 1, cut_two, links)
-        retain(b)
         if following:
             gather_flat(b + 1, cells, whole)
             reduce_start(b + 1)
@@ -637,6 +683,7 @@
         gather_drain(b)
         reduce_drain(b)
         share_drain(b)
+        pltpu.make_async_copy(out_ref.at[b], out_hbm.at[b], out_sem.at[b]).wait()
 
 
 def on_device(start_block, resident, stiffness, cell_scale, potential, cell_count, face_index):
@@ -652,12 +699,16 @@
     dma = pltpu.SemaphoreType.DMA
     vmem = pl.BlockSpec(memory_space=pltpu.VMEM)
     smem = pl.BlockSpec(memory_space=pltpu.SMEM)
+    anywhere = pl.BlockSpec(memory_space=pl.ANY)
     return pl.pallas_call(
         partial(kernel, sizes),
         out_shape=jax.ShapeDtypeStruct((blocks, cells, width, nodes), BF16),
-        in_specs=[smem, smem, vmem, pl.BlockSpec(memory_space=pl.ANY), vmem, vmem, vmem],
-        out_specs=vmem,
+        in_specs=[smem, smem, anywhere, anywhere, anywhere, vmem, vmem],
+        out_specs=anywhere,
         scratch_shapes=[
+            pltpu.VMEM((blocks, cells, width, nodes), BF16),
+            pltpu.VMEM((nodes, nodes), BF16),
+            pltpu.VMEM((blocks, cells, width, nodes), BF16),
             pltpu.VMEM((blocks, cells * width, nodes), F32),
             pltpu.VMEM((blocks, cells * width, nodes), BF16),
             pltpu.VMEM((blocks, cells, total_states, nodes), BF16),
@@ -687,7 +738,10 @@
             dma((blocks, doms)),
             dma((blocks, sts)),
             dma((2, blocks, sts, cells)),
-            dma,
+            dma((4,)),
+            dma((blocks,)),
+            dma((2,)),
+            dma((blocks,)),
             dma((2, near)),
             dma((2, near)),
             dma((2, blocks)),

time: 114 us -> 105 us (0.921)
  Pallas kernels: 111 us -> 102 us
    pallas_call x1, Pallas kernels: 111 us -> 102 us  [on_device(): pl.pallas_call(partial(kernel, sizes), out_shape=jax.ShapeDtypeStruct((bl...]
where the time goes in v2:
time: 105 us
  Pallas kernels  102 us (97%)
  local copies, waits for them, and re-layouts  2.06 us (2%)
    pallas_call x1, Pallas kernels, on_device(): pl.pallas_call(partial(kernel, sizes), out_shape=jax.ShapeDtypeStruct((bl...  102 us

profile of v2, /device:TPU:0, one launch (start us, length us, event | category | flops | bytes accessed | tf_op | source)
XLA Modules:
  0.0 105.2 jit_solution(4899539148919167125)
XLA Ops:
  0.7 102.5 %shard_map.73 = bf16[2,8,32,729]{3,2,1,0:T(8,128)(2,1)} custom-call(f32[8]{0:T(128)} %scale_ref.1, s32[1]{0:T(128)S(6)} %copy.9.count_ref, bf16[2,8,32,729]{3,2,1,0:T(8,128)(2,1)} %start_hbm.1, bf16[729,8,256]{2,1,0:T(8,128)(2,1)} %bitcast.1, bf16[729,729]{1,0:T(8,128)(2,1)} %stiff_hbm.1, f32[8,729]{1,0:T(8,128)} %pot_ref.1, s32[1,2,81]{2,1,0:T(2,128)} %face_ref.1), custom_call_target="tpu_custom_call" | custom-call | tf_op jit(solution)/shard_map/pallas_call | solution.py:703
  103.1 2.1 %copy.10 = bf16[2,8,32,729]{3,2,1,0:T(8,128)(2,1)} copy(bf16[2,8,32,729]{3,2,1,0:T(8,128)(2,1)} %shard_map.73) | data formatting | bytes 1492992

commit v3 on v2

--- a/solution.py
+++ b/solution.py
@@ -14,7 +14,7 @@
 BF16 = jnp.bfloat16
 WIRE = BF16
 RIGHT, LEFT = 0, 1
-LAG = 3
+LAG = 6
 MESH = pl.DeviceIdType.MESH
 
 
@@ -67,6 +67,10 @@
     res_near,
     proj_near,
     retained,
+    near_part,
+    near_wire,
+    near_got,
+    near_term,
     face_out,
     face_in,
     face_send_sem,
@@ -87,8 +91,10 @@
     near_recv_sem,
     coef_send_sem,
     coef_recv_sem,
+    give_send_sem,
+    give_recv_sem,
 ):
-    doms, sts, blocks, cells, width, nodes, face, res, rows, moved = sizes
+    doms, sts, blocks, cells, width, nodes, face, res, rows, moved, given = sizes
     total_states = sts * width
     total_nodes = float(doms * cells * nodes)
     window = (nodes - face) // 128 * 128
@@ -132,9 +138,14 @@
 
     origin = {RIGHT: s == 0, LEFT: s == steps}
     lag = {RIGHT: LAG * jnp.maximum(s - 1, 0), LEFT: LAG * jnp.maximum(steps - 1 - s, 0)}
+    done_at = jnp.maximum(
+        jnp.where(s > 0, lag[RIGHT] + (steps - s) * cells, 0),
+        jnp.where(s < steps, lag[LEFT] + s * cells, 0),
+    )
     sends = {RIGHT: has_right, LEFT: has_left}
     receives = {RIGHT: has_left, LEFT: has_right}
     near_end = {RIGHT: s == 1, LEFT: s == steps - 1}
+    to_end = {RIGHT: s == steps - 1, LEFT: s == 1}
 
     def to(way):
         return s + 1 if way == RIGHT else s - 1
@@ -283,8 +294,8 @@
             at, at, gather_send_sem.at[b, way, shard], gather_recv_sem.at[b, shard, c], "st", to(way)
         )
 
-    def gather_whole(b, way, shard):
-        at = states.at[b, :, of_shard(shard), :]
+    def gather_whole(b, way, shard, begin):
+        at = states.at[b, pl.ds(begin, cells - begin), of_shard(shard), :]
         return remote(
             at, at, gather_send_sem.at[b, way, shard], gather_recv_sem.at[b, shard, 0], "st", to(way)
         )
@@ -296,29 +307,41 @@
                 gather_copy(b, way, s, c).start()
                 return carry
 
-            lax.fori_loop(0, cells, one, 0)
+            lax.fori_loop(jnp.where(to_end[way], given[b], 0), cells, one, 0)
 
     def gather_start(b, k):
         gather_own(b, RIGHT, s == k)
         gather_own(b, LEFT, s + k == steps)
 
     def gather_flat(b, begin, end):
+        wait = min(5, cells - given[b])
+
         def one(i, carry):
             k = lax.div(i, cells) + 1
             c = lax.rem(i, cells)
+            whole = both(c >= given[b])
+            held = jnp.logical_or(whole, jnp.logical_not(ends))
             for way, shard, here in ((LEFT, s + k, s + k < sts), (RIGHT, s - k, s >= k)):
-
-                @pl.when(here)
+                passed = jnp.logical_or(whole, jnp.logical_not(to_end[way]))
+
+                @pl.when(both(here, held))
                 def _():
                     gather_copy(b, way, shard, c).wait_recv()
 
-                    @pl.when(sends[way])
+                    @pl.when(both(sends[way], passed))
                     def _():
                         gather_copy(b, way, shard, c).start()
 
-            @pl.when(k == last_step)
+            @pl.when(both(k == last_step, held))
             def _():
                 contract(b, c)
+
+            if given[b]:
+                for way in (RIGHT, LEFT):
+
+                    @pl.when(both(k == last_step, near_end[way], c >= wait, c < wait + given[b]))
+                    def _():
+                        contract_near(b, way, c - wait)
 
             if b + 1 < blocks:
 
@@ -334,9 +357,13 @@
         def one(shard, carry):
             for way, passed in ((RIGHT, shard <= s), (LEFT, shard >= s)):
 
-                @pl.when(both(passed, sends[way]))
+                @pl.when(both(passed, sends[way], to_end[way]))
                 def _():
-                    gather_whole(b, way, shard).wait_send()
+                    gather_whole(b, way, shard, given[b]).wait_send()
+
+                @pl.when(both(passed, sends[way], jnp.logical_not(to_end[way])))
+                def _():
+                    gather_whole(b, way, shard, 0).wait_send()
 
             return carry
 
@@ -350,6 +377,55 @@
             at = slice(h * total_states, (h + 1) * total_states)
             part[b, at, :] += found[:, at]
         part[b, res : res + total_states, :] += dot_nt(block, block)
+
+    def give_copy(b, way):
+        return remote(
+            near_wire.at[b],
+            near_got.at[b],
+            give_send_sem.at[b],
+            give_recv_sem.at[b],
+            "st",
+            to(1 - way),
+        )
+
+    def contract_near(b, way, c):
+        @pl.when(c >= (given[b - 1] if b else 0))
+        def _():
+            near_wait(way, c)
+
+        @pl.when(c == 0)
+        def _():
+            near_part[b] = jnp.zeros(near_part.shape[1:], F32)
+
+        block = states[b, c]
+        found = dot_nn(block, res_near[way, c])
+        for h in range(res // total_states):
+            at = slice(h * total_states, (h + 1) * total_states)
+            near_part[b, at, :] += found[:, at]
+        near_part[b, res : res + total_states, :] += dot_nt(block, block)
+
+        @pl.when(c == given[b] - 1)
+        def _():
+            near_wire[b] = near_part[b].astype(WIRE)
+            give_copy(b, way).start()
+
+    def give_end(b):
+        if not given[b]:
+            return
+        at = slice(0, res + total_states)
+
+        @pl.when(ends)
+        def _():
+            give_copy(b, RIGHT).wait_recv()
+            part[b, at, :] += near_got[b].astype(F32)
+
+    def give_drain(b):
+        if not given[b]:
+            return
+
+        @pl.when(jnp.logical_or(near_end[RIGHT], near_end[LEFT]))
+        def _():
+            give_copy(b, RIGHT).wait_send()
 
     def slice_of(peer):
         return pl.ds(pl.multiple_of(peer * rows, 16), rows)
@@ -382,6 +458,7 @@
         lax.fori_loop(1, doms, step, 0)
 
     def reduce_start(b):
+        give_end(b)
         wire[b] = part[b].astype(WIRE)
         peers(lambda k: one_copy(b, k).start())
 
@@ -422,17 +499,18 @@
             ).astype(BF16)
 
 
-    def near_copy(way, c):
+    def near_copy(way, c, i):
+        at = cuts(nodes, 2)[i]
         return remote(
-            res_ref.at[c],
-            res_near.at[way, c],
-            near_send_sem.at[way, c],
-            near_recv_sem.at[way, c],
+            res_ref.at[c, at],
+            res_near.at[way, c, at],
+            near_send_sem.at[way, c, i],
+            near_recv_sem.at[way, c, i],
             "st",
             to(way),
         )
 
-    def near_start(c):
+    def near_start(c, i):
         if c >= moved:
             return
         for way in (RIGHT, LEFT):
@@ -440,9 +518,13 @@
 
             @pl.when(there)
             def _():
-                near_copy(way, c).start()
-
-            pending.append((there, partial(near_copy, way, c)))
+                near_copy(way, c, i).start()
+
+            pending.append((there, partial(near_copy, way, c, i)))
+
+    def near_wait(way, c):
+        for i in range(2):
+            near_copy(way, c, i).wait_recv()
 
     def coef_copy(b, way):
         return remote(
@@ -509,25 +591,44 @@
     def share_start(b):
         def one(i, carry):
             c = lax.rem(i + moved, cells)
-            share_cell(b, c)
+
+            @pl.when(c < given[b])
+            def _():
+                retained[b, c] = jnp.zeros(retained.shape[2:], F32)
+
+            @pl.when(c >= given[b])
+            def _():
+                share_cell(b, c)
+
             for way in (RIGHT, LEFT):
 
                 @pl.when(both(origin[way], c >= moved))
                 def _():
-                    number, target = ahead(way)
-
-                    def send(i, carry):
-                        share_copy(b, target(i), way, c).start()
-                        return carry
-
-                    lax.fori_loop(0, number, send, 0)
-
-            retain(b, c)
+                    share_copy(b, ahead(way)[1](0), way, c).start()
+
+            @pl.when(c >= given[b])
+            def _():
+                retain(b, c)
+
             return carry
 
+        def rest(i, carry):
+            for way in (RIGHT, LEFT):
+
+                @pl.when(origin[way])
+                def _():
+                    t = ahead(way)[1](lax.div(i, kept) + 1)
+                    share_copy(b, t, way, lax.rem(i, kept) + moved).start()
+
+            return carry
+
+        kept = cells - moved
+
         @pl.when(ends)
         def _():
-            lax.fori_loop(0, cells, one, 0)
+            lax.fori_loop(0, kept, one, 0)
+            lax.fori_loop(0, (steps - 1) * kept, rest, 0)
+            lax.fori_loop(kept, cells, one, 0)
 
     def share_drain(b):
         def one(t, carry):
@@ -545,38 +646,51 @@
 
         lax.fori_loop(0, sts, one, 0)
 
-    def absorb(b, way, c):
-        number, target = ahead(way)
-
-        def one(i, carry):
-            t = target(i)
-            share_copy(b, t, way, c).wait_recv()
-            share[b, t, c] = (
-                share[b, t, c].astype(F32) + share_recv[way, b, t, c].astype(F32)
-            ).astype(BF16)
+    def absorb(b, way, t, c):
+        share_copy(b, t, way, c).wait_recv()
+
+        @pl.when(t == s)
+        def _():
+            retained[b, c] -= share_recv[way, b, t, c].astype(F32)
+
+        @pl.when(t != s)
+        def _():
+            found = share[b, t, c].astype(F32) + share_recv[way, b, t, c].astype(F32)
+            share[b, t, c] = found.astype(BF16)
+            if given[b]:
+
+                @pl.when(both(to_end[way], c < given[b]))
+                def _():
+                    share[b, t, c] = (found + near_term[b, c]).astype(BF16)
+
             share_copy(b, t, way, c).start()
-            return carry
-
-        lax.fori_loop(0, number, one, 0)
-        share_copy(b, s, way, c).wait_recv()
-        retained[b, c] -= share_recv[way, b, s, c].astype(F32)
 
     def absorb_near(b, way, c):
         if b == 0:
-            near_copy(way, c).wait_recv()
+
+            @pl.when(c >= max(given))
+            def _():
+                near_wait(way, c)
 
         @pl.when(c == 0)
         def _():
             coef_copy(b, way).wait_recv()
 
         found = dot_nt(proj_near[way, b], res_near[way, c])
+        if given[b]:
+
+            @pl.when(c < given[b])
+            def _():
+                at = (0 if way == RIGHT else steps) * width
+                end = slice(at, at + width)
+                near_term[b, c] = found[end, :] - dot_nn(mix[b, end, :], states[b, c])
+
         for t in reversed(range(sts)) if way == RIGHT else range(sts):
             piece = found[t * width : (t + 1) * width, :]
 
             @pl.when(t > s if way == RIGHT else t < s)
             def _():
                 share[b, t, c] = (share[b, t, c].astype(F32) + piece).astype(BF16)
-                share_copy(b, t, way, c).start()
 
             @pl.when(t == s)
             def _():
@@ -584,28 +698,33 @@
 
     def chain(b, begin, end):
         def one(j, carry):
-            c = j
-
-            @pl.when(both(jnp.logical_not(ends), c >= 0, c < cells))
-            def _():
-                share_cell(b, c)
-                retain(b, c)
+            @pl.when(both(jnp.logical_not(ends), j < cells))
+            def _():
+                share_cell(b, j)
+                retain(b, j)
 
             for way in (RIGHT, LEFT):
-                c = j - lag[way]
-                here = both(receives[way], c >= 0, c < cells)
+                m = j - lag[way]
+                i = lax.div(jnp.maximum(m, 0), cells)
+                c = lax.rem(jnp.maximum(m, 0), cells)
+                number, target = ahead(way)
+                here = both(receives[way], m >= 0, i <= number)
                 near = both(near_end[way], c < moved)
                 if moved:
 
-                    @pl.when(both(here, near))
+                    @pl.when(both(here, near, i == 0))
                     def _():
                         absorb_near(b, way, c)
 
+                    @pl.when(both(here, near, i < number))
+                    def _():
+                        share_copy(b, target(i), way, c).start()
+
                 @pl.when(both(here, jnp.logical_not(near)))
                 def _():
-                    absorb(b, way, c)
-
-            c = j - jnp.maximum(lag[RIGHT], lag[LEFT])
+                    absorb(b, way, target(i), c)
+
+            c = j - done_at
 
             @pl.when(both(c >= 0, c < cells))
             def _():
@@ -629,7 +748,7 @@
         operator_begin(0, b)
         if b == 0:
             relayout()
-            near_start(0)
+            near_start(0, 0)
     for b in range(blocks):
         operator_end(0, b)
         operator_begin(1, b)
@@ -638,17 +757,20 @@
         if b == 0:
             for k in range(sts):
                 gather_start(0, k)
-            near_start(1)
+            near_start(0, 1)
+            for i in range(2):
+                near_start(1, i)
         if b == 1:
             gather_start(1, 0)
     for c in range(2, moved):
-        near_start(c)
+        for i in range(2):
+            near_start(c, i)
 
     half = cells // 2
     whole = steps * cells
-    furthest = LAG * max(steps - 1, 0)
-    links = cells + furthest
-    cut_one, cut_two = furthest + 2, furthest + 6
+    links = done_at + cells
+    cut_one = jnp.where(ends, done_at, cells // 2)
+    cut_two = jnp.where(ends, done_at + 2, cells)
     gather_flat(0, 0, whole)
     reduce_start(0)
     for b in range(blocks):
@@ -683,6 +805,7 @@
         gather_drain(b)
         reduce_drain(b)
         share_drain(b)
+        give_drain(b)
         pltpu.make_async_copy(out_ref.at[b], out_hbm.at[b], out_sem.at[b]).wait()
 
 
@@ -694,7 +817,8 @@
     total_states = sts * width
     rows = -(-(res + total_states) // (16 * doms)) * 16
     moved = 3 * cells // 8 if sts > 3 else 0
-    sizes = (doms, sts, blocks, cells, width, nodes, face, res, rows, moved)
+    given = tuple(min(moved, (2 * b + 1) * cells // 8) for b in range(blocks))
+    sizes = (doms, sts, blocks, cells, width, nodes, face, res, rows, moved, given)
     near = max(moved, 1)
     dma = pltpu.SemaphoreType.DMA
     vmem = pl.BlockSpec(memory_space=pltpu.VMEM)
@@ -726,6 +850,10 @@
             pltpu.VMEM((2, near, nodes, res), BF16),
             pltpu.VMEM((2, blocks, total_states, res), BF16),
             pltpu.VMEM((blocks, cells, width, nodes), F32),
+            pltpu.VMEM((blocks, res + total_states, total_states), F32),
+            pltpu.VMEM((blocks, res + total_states, total_states), WIRE),
+            pltpu.VMEM((blocks, res + total_states, total_states), WIRE),
+            pltpu.VMEM((blocks, near, width, nodes), F32),
             pltpu.VMEM((2, blocks, 2, width, face), F32),
             pltpu.VMEM((2, blocks, 2, width, face), F32),
             dma((2, blocks, 2)),
@@ -742,10 +870,12 @@
             dma((blocks,)),
             dma((2,)),
             dma((blocks,)),
-            dma((2, near)),
-            dma((2, near)),
+            dma((2, near, 2)),
+            dma((2, near, 2)),
             dma((2, blocks)),
             dma((2, blocks)),
+            dma((blocks,)),
+            dma((blocks,)),
         ],
         compiler_params=pltpu.CompilerParams(
             collective_id=0, has_side_effects=True, vmem_limit_bytes=60 * 1024 * 1024

time: 105 us -> 99.1 us (0.944)
  the two profiles are of different devices: /device:TPU:0 before, /device:TPU:10 now
where the time goes in v3:
time: 99.1 us; the launch traced here: 97.5 us
  Pallas kernels  94.8 us (96%)
  local copies, waits for them, and re-layouts  2.06 us (2%)
    pallas_call x1, Pallas kernels, on_device(): pl.pallas_call(partial(kernel, sizes), out_shape=jax.ShapeDtypeStruct((bl...  94.8 us
    unnamed x1, local copies, waits for them, and re-layouts  2.06 us

profile of v3, /device:TPU:10, one launch (start us, length us, event | category | flops | bytes accessed | tf_op | source)
XLA Modules:
  0.0 97.5 jit_solution(10173874016176112042)
XLA Ops:
  0.7 94.8 %shard_map.73 = bf16[2,8,32,729]{3,2,1,0:T(8,128)(2,1)} custom-call(f32[8]{0:T(128)} %scale_ref.1, s32[1]{0:T(128)S(6)} %copy.9.count_ref, bf16[2,8,32,729]{3,2,1,0:T(8,128)(2,1)} %start_hbm.1, bf16[729,8,256]{2,1,0:T(8,128)(2,1)} %bitcast.1, bf16[729,729]{1,0:T(8,128)(2,1)} %stiff_hbm.1, f32[8,729]{1,0:T(8,128)} %pot_ref.1, s32[1,2,81]{2,1,0:T(2,128)} %face_ref.1), custom_call_target="tpu_custom_call" | custom-call | tf_op jit(solution)/shard_map/pallas_call | solution.py:827
  95.4 2.1 %copy.10 = bf16[2,8,32,729]{3,2,1,0:T(8,128)(2,1)} copy(bf16[2,8,32,729]{3,2,1,0:T(8,128)(2,1)} %shard_map.73) | data formatting | bytes 1492992

commit v4 on v3

--- a/solution.py
+++ b/solution.py
@@ -120,21 +120,19 @@
         step = -(-extent // (number * 16)) * 16
         return [pl.ds(at, min(step, extent - at)) for at in range(0, extent, step)]
 
-    def stiff_load(i):
-        at = cuts(nodes, 2)[i]
-        return pltpu.make_async_copy(stiff_hbm.at[at], stiff_ref.at[at], stiff_sem.at[i])
-
-    def res_load(i):
-        at = cuts(nodes, 4)[i]
-        return pltpu.make_async_copy(res_hbm.at[at], res_in.at[at], load_sem.at[i])
+    def stiff_load(at):
+        return pltpu.make_async_copy(stiff_hbm.at[at], stiff_ref.at[at], stiff_sem)
+
+    def res_load(at):
+        return pltpu.make_async_copy(res_hbm.at[at], res_in.at[at], load_sem)
 
     start_load(0).start()
-    for i in range(2):
-        stiff_load(i).start()
+    for at in cuts(nodes, 2):
+        stiff_load(at).start()
     for b in range(1, blocks):
         start_load(b).start()
-    for i in range(4):
-        res_load(i).start()
+    for at in cuts(nodes, 4):
+        res_load(at).start()
 
     origin = {RIGHT: s == 0, LEFT: s == steps}
     lag = {RIGHT: LAG * jnp.maximum(s - 1, 0), LEFT: LAG * jnp.maximum(steps - 1 - s, 0)}
@@ -166,8 +164,9 @@
         def _():
             pl.semaphore_signal(barrier, inc=1, device_id={"st": to(way)}, device_id_type=MESH)
 
-    neighbours = has_right.astype(jnp.int32) + has_left.astype(jnp.int32)
-    pl.semaphore_wait(barrier, doms - 1 + neighbours)
+    def meet():
+        neighbours = has_right.astype(jnp.int32) + has_left.astype(jnp.int32)
+        pl.semaphore_wait(barrier, doms - 1 + neighbours)
 
     def remote(src, dst, send_sem, recv_sem, axis, peer):
         return pltpu.make_async_remote_copy(
@@ -189,8 +188,7 @@
         return live[c].astype(BF16)
 
     def relayout():
-        for i in range(4):
-            res_load(i).wait()
+        res_load(pl.ds(0, nodes)).wait()
         for chunk in range(nodes // face):
             at = slice(chunk * face, (chunk + 1) * face)
             wide = res_in[at].astype(F32).reshape(face * cells, res)
@@ -222,7 +220,7 @@
     def second(b, c):
         return inner[b] if c is None else inner[b, rows_of(c), :]
 
-    def operator_begin(step, b):
+    def operator_begin(step, b, meanwhile=None):
         field = partial(second if step else first, b)
         local[b] = dot_nn(field(None), stiff_ref[...])
         last_tail = jnp.zeros((width, nodes - window), F32)
@@ -236,6 +234,8 @@
         face_out[step, b, LEFT] = dot_nn(
             local[b, rows_of(0), :face], one_hot(1, 0, face), lax.Precision.HIGHEST
         )
+        if meanwhile is not None:
+            meanwhile()
         for way, there in ((RIGHT, has_next), (LEFT, has_prev)):
 
             @pl.when(there)
@@ -288,23 +288,24 @@
     def of_shard(shard):
         return pl.ds(pl.multiple_of(shard * width, width), width)
 
-    def gather_copy(b, way, shard, c):
+    def gather_copy(b, way, shard, c, here):
         at = states.at[b, c, of_shard(shard), :]
+        slot = jnp.where(shard > here, shard - 1, shard)
         return remote(
-            at, at, gather_send_sem.at[b, way, shard], gather_recv_sem.at[b, shard, c], "st", to(way)
+            at, at, gather_send_sem.at[b, way, shard], gather_recv_sem.at[b, slot, c], "st", to(way)
         )
 
     def gather_whole(b, way, shard, begin):
         at = states.at[b, pl.ds(begin, cells - begin), of_shard(shard), :]
         return remote(
-            at, at, gather_send_sem.at[b, way, shard], gather_recv_sem.at[b, shard, 0], "st", to(way)
+            at, at, gather_send_sem.at[b, way, shard], gather_recv_sem.at[b, 0, 0], "st", to(way)
         )
 
     def gather_own(b, way, there):
         @pl.when(both(there, sends[way]))
         def _():
             def one(c, carry):
-                gather_copy(b, way, s, c).start()
+                gather_copy(b, way, s, c, to(way)).start()
                 return carry
 
             lax.fori_loop(jnp.where(to_end[way], given[b], 0), cells, one, 0)
@@ -326,11 +327,11 @@
 
                 @pl.when(both(here, held))
                 def _():
-                    gather_copy(b, way, shard, c).wait_recv()
+                    gather_copy(b, way, shard, c, s).wait_recv()
 
                     @pl.when(both(sends[way], passed))
                     def _():
-                        gather_copy(b, way, shard, c).start()
+                        gather_copy(b, way, shard, c, to(way)).start()
 
             @pl.when(both(k == last_step, held))
             def _():
@@ -435,20 +436,24 @@
         return remote(
             wire.at[b, slice_of(peer)],
             part_recv.at[b, k],
-            one_send_sem.at[b, k],
-            one_recv_sem.at[b, k],
+            one_send_sem.at[b],
+            one_recv_sem.at[b],
             "dom",
             peer,
         )
 
     def two_copy(b, k):
         at = total.at[b, slice_of(d)]
-        return remote(at, at, two_send_sem.at[b, k], two_recv_sem.at[b, k], "dom", dom_peer(k))
-
-    def from_peer(b, k):
-        peer = dom_peer(doms - k)
-        at = total.at[b, slice_of(peer)]
-        return remote(at, at, two_send_sem.at[b, k], two_recv_sem.at[b, k], "dom", peer)
+        return remote(at, at, two_send_sem.at[b], two_recv_sem.at[b], "dom", dom_peer(k))
+
+
+    def one_whole(b):
+        at = part_recv.at[b, pl.ds(1, doms - 1)]
+        return remote(at, at, one_send_sem.at[b], one_recv_sem.at[b], "dom", dom_peer(1))
+
+    def two_whole(b):
+        at = total.at[b, pl.ds(0, (doms - 1) * rows)]
+        return remote(at, at, two_send_sem.at[b], two_recv_sem.at[b], "dom", dom_peer(1))
 
     def peers(body):
         def step(k, carry):
@@ -463,8 +468,9 @@
         peers(lambda k: one_copy(b, k).start())
 
     def reduce_middle(b):
+        one_whole(b).wait_recv()
+
         def add(k, found):
-            one_copy(b, k).wait_recv()
             return found + part_recv[b, k].astype(F32)
 
         found = lax.fori_loop(1, doms, add, part[b, slice_of(d), :])
@@ -472,14 +478,11 @@
         peers(lambda k: two_copy(b, k).start())
 
     def reduce_end(b):
-        peers(lambda k: from_peer(b, k).wait_recv())
+        two_whole(b).wait_recv()
 
     def reduce_drain(b):
-        def one(k):
-            one_copy(b, k).wait_send()
-            two_copy(b, k).wait_send()
-
-        peers(one)
+        one_whole(b).wait_send()
+        two_whole(b).wait_send()
 
     def coefficients(b):
         gram = total[b, res : res + total_states, :].astype(F32)
@@ -504,8 +507,8 @@
         return remote(
             res_ref.at[c, at],
             res_near.at[way, c, at],
-            near_send_sem.at[way, c, i],
-            near_recv_sem.at[way, c, i],
+            near_send_sem.at[c, i],
+            near_recv_sem.at[c, i],
             "st",
             to(way),
         )
@@ -530,8 +533,8 @@
         return remote(
             proj.at[b],
             proj_near.at[way, b],
-            coef_send_sem.at[way, b],
-            coef_recv_sem.at[way, b],
+            coef_send_sem.at[b],
+            coef_recv_sem.at[b],
             "st",
             to(way),
         )
@@ -549,12 +552,13 @@
             pending.append((there, partial(coef_copy, b, way)))
 
 
-    def share_copy(b, t, way, c):
+    def share_copy(b, t, way, c, here):
+        slot = jnp.where(jnp.logical_and(t == here, way == LEFT), sts, t)
         return remote(
             share.at[b, t, c],
             share_recv.at[way, b, t, c],
             share_send_sem.at[b, t],
-            share_recv_sem.at[way, b, t, c],
+            share_recv_sem.at[b, slot, c],
             "st",
             to(way),
         )
@@ -565,7 +569,7 @@
             share.at[b, t, at],
             share_recv.at[way, b, t, at],
             share_send_sem.at[b, t],
-            share_recv_sem.at[way, b, t, 0],
+            share_recv_sem.at[b, t, 0],
             "st",
             to(way),
         )
@@ -604,7 +608,7 @@
 
                 @pl.when(both(origin[way], c >= moved))
                 def _():
-                    share_copy(b, ahead(way)[1](0), way, c).start()
+                    share_copy(b, ahead(way)[1](0), way, c, to(way)).start()
 
             @pl.when(c >= given[b])
             def _():
@@ -618,7 +622,7 @@
                 @pl.when(origin[way])
                 def _():
                     t = ahead(way)[1](lax.div(i, kept) + 1)
-                    share_copy(b, t, way, lax.rem(i, kept) + moved).start()
+                    share_copy(b, t, way, lax.rem(i, kept) + moved, to(way)).start()
 
             return carry
 
@@ -647,7 +651,7 @@
         lax.fori_loop(0, sts, one, 0)
 
     def absorb(b, way, t, c):
-        share_copy(b, t, way, c).wait_recv()
+        share_copy(b, t, way, c, s).wait_recv()
 
         @pl.when(t == s)
         def _():
@@ -663,7 +667,7 @@
                 def _():
                     share[b, t, c] = (found + near_term[b, c]).astype(BF16)
 
-            share_copy(b, t, way, c).start()
+            share_copy(b, t, way, c, to(way)).start()
 
     def absorb_near(b, way, c):
         if b == 0:
@@ -696,59 +700,61 @@
             def _():
                 retained[b, c] -= piece
 
-    def chain(b, begin, end):
+    def chain(turns, begin, end):
         def one(j, carry):
-            @pl.when(both(jnp.logical_not(ends), j < cells))
-            def _():
-                share_cell(b, j)
-                retain(b, j)
-
-            for way in (RIGHT, LEFT):
-                m = j - lag[way]
-                i = lax.div(jnp.maximum(m, 0), cells)
-                c = lax.rem(jnp.maximum(m, 0), cells)
-                number, target = ahead(way)
-                here = both(receives[way], m >= 0, i <= number)
-                near = both(near_end[way], c < moved)
-                if moved:
-
-                    @pl.when(both(here, near, i == 0))
-                    def _():
-                        absorb_near(b, way, c)
-
-                    @pl.when(both(here, near, i < number))
-                    def _():
-                        share_copy(b, target(i), way, c).start()
-
-                @pl.when(both(here, jnp.logical_not(near)))
-                def _():
-                    absorb(b, way, target(i), c)
-
-            c = j - done_at
-
-            @pl.when(both(c >= 0, c < cells))
-            def _():
-                alive = jnp.where(c < count, 1.0, 0.0).astype(BF16)
-                out_ref[b, c] = retained[b, c].astype(BF16) * alive
-                pltpu.make_async_copy(out_ref.at[b, c], out_hbm.at[b, c], out_sem.at[b]).start()
-
+            for b, offset in turns:
+                chain_step(b, j + offset)
             return carry
 
         lax.fori_loop(begin, end, one, 0)
+
+    def chain_step(b, j):
+        @pl.when(both(jnp.logical_not(ends), j < cells))
+        def _():
+            share_cell(b, j)
+            retain(b, j)
+
+        for way in (RIGHT, LEFT):
+            m = j - lag[way]
+            i = lax.div(jnp.maximum(m, 0), cells)
+            c = lax.rem(jnp.maximum(m, 0), cells)
+            number, target = ahead(way)
+            here = both(receives[way], m >= 0, i <= number)
+            near = both(near_end[way], c < moved)
+            if moved:
+
+                @pl.when(both(here, near, i == 0))
+                def _():
+                    absorb_near(b, way, c)
+
+                @pl.when(both(here, near, i < number))
+                def _():
+                    share_copy(b, target(i), way, c, to(way)).start()
+
+            @pl.when(both(here, jnp.logical_not(near)))
+            def _():
+                absorb(b, way, target(i), c)
+
+        c = j - done_at
+
+        @pl.when(both(c >= 0, c < cells))
+        def _():
+            alive = jnp.where(c < count, 1.0, 0.0).astype(BF16)
+            out_ref[b, c] = retained[b, c].astype(BF16) * alive
+            pltpu.make_async_copy(out_ref.at[b, c], out_hbm.at[b, c], out_sem.at[b]).start()
 
 
     for b in range(blocks):
         part[b] = jnp.zeros(part.shape[1:], F32)
     start_load(0).wait()
+    stiff_load(pl.ds(0, nodes)).wait()
+    operator_begin(0, 0, meet)
+    relayout()
     for i in range(2):
-        stiff_load(i).wait()
-    for b in range(blocks):
-        if b:
-            start_load(b).wait()
+        near_start(0, i)
+    for b in range(1, blocks):
+        start_load(b).wait()
         operator_begin(0, b)
-        if b == 0:
-            relayout()
-            near_start(0, 0)
     for b in range(blocks):
         operator_end(0, b)
         operator_begin(1, b)
@@ -757,7 +763,6 @@
         if b == 0:
             for k in range(sts):
                 gather_start(0, k)
-            near_start(0, 1)
             for i in range(2):
                 near_start(1, i)
         if b == 1:
@@ -769,6 +774,7 @@
     half = cells // 2
     whole = steps * cells
     links = done_at + cells
+    over = 3 * cells // 4
     cut_one = jnp.where(ends, done_at, cells // 2)
     cut_two = jnp.where(ends, done_at + 2, cells)
     gather_flat(0, 0, whole)
@@ -778,22 +784,23 @@
         if following:
             gather_flat(b + 1, 0, half)
         if previous:
-            chain(b - 1, 0, cut_one)
+            chain([(b - 1, 0)], over if b > 1 else 0, cut_one)
         reduce_middle(b)
         if following:
             gather_flat(b + 1, half, cells)
         if previous:
-            chain(b - 1, cut_one, cut_two)
+            chain([(b - 1, 0)], cut_one, cut_two)
         reduce_end(b)
         coefficients(b)
         coef_start(b)
         share_start(b)
         if previous:
-            chain(b - 1, cut_two, links)
+            chain([(b - 1, 0)], cut_two, links - over)
+            chain([(b - 1, links - over), (b, 0)], 0, over)
         if following:
             gather_flat(b + 1, cells, whole)
             reduce_start(b + 1)
-    chain(blocks - 1, 0, links)
+    chain([(blocks - 1, 0)], over if blocks > 1 else 0, links)
 
     for there, make in pending:
 
@@ -859,21 +866,21 @@
             dma((2, blocks, 2)),
             dma((2, blocks, 2)),
             dma((blocks, 2, sts)),
-            dma((blocks, sts, cells)),
-            dma((blocks, doms)),
-            dma((blocks, doms)),
-            dma((blocks, doms)),
-            dma((blocks, doms)),
+            dma((blocks, max(sts - 1, 1), cells)),
+            dma((blocks,)),
+            dma((blocks,)),
+            dma((blocks,)),
+            dma((blocks,)),
             dma((blocks, sts)),
-            dma((2, blocks, sts, cells)),
-            dma((4,)),
+            dma((blocks, sts + 1, cells)),
+            dma,
             dma((blocks,)),
-            dma((2,)),
+            dma,
             dma((blocks,)),
-            dma((2, near, 2)),
-            dma((2, near, 2)),
-            dma((2, blocks)),
-            dma((2, blocks)),
+            dma((near, 2)),
+            dma((near, 2)),
+            dma((blocks,)),
+            dma((blocks,)),
             dma((blocks,)),
             dma((blocks,)),
         ],

time: 99.1 us -> 93.6 us (0.945); the launches traced: 97.5 us -> 93.4 us
  Pallas kernels: 94.8 us -> 90.7 us
    pallas_call x1, Pallas kernels: 94.8 us -> 90.7 us  [on_device(): pl.pallas_call(partial(kernel, sizes), out_shape=jax.ShapeDtypeStruct((bl...]
where the time goes in v4:
time: 93.6 us; the launch traced here: 93.4 us
  Pallas kernels  90.7 us (97%)
  local copies, waits for them, and re-layouts  2.06 us (2%)
    pallas_call x1, Pallas kernels, on_device(): pl.pallas_call(partial(kernel, sizes), out_shape=jax.ShapeDtypeStruct((bl...  90.7 us
    unnamed x1, local copies, waits for them, and re-layouts  2.06 us

profile of v4, /device:TPU:10, one launch (start us, length us, event | category | flops | bytes accessed | tf_op | source)
XLA Modules:
  0.0 93.4 jit_solution(6944013024029196669)
XLA Ops:
  0.7 90.7 %shard_map.73 = bf16[2,8,32,729]{3,2,1,0:T(8,128)(2,1)} custom-call(f32[8]{0:T(128)} %scale_ref.1, s32[1]{0:T(128)S(6)} %copy.9.count_ref, bf16[2,8,32,729]{3,2,1,0:T(8,128)(2,1)} %start_hbm.1, bf16[729,8,256]{2,1,0:T(8,128)(2,1)} %bitcast.1, bf16[729,729]{1,0:T(8,128)(2,1)} %stiff_hbm.1, f32[8,729]{1,0:T(8,128)} %pot_ref.1, s32[1,2,81]{2,1,0:T(2,128)} %face_ref.1), custom_call_target="tpu_custom_call" | custom-call | tf_op jit(solution)/shard_map/pallas_call | solution.py:834
  91.4 2.1 %copy.10 = bf16[2,8,32,729]{3,2,1,0:T(8,128)(2,1)} copy(bf16[2,8,32,729]{3,2,1,0:T(8,128)(2,1)} %shard_map.73) | data formatting | bytes 1492992

commit v5 on v4

--- a/solution.py
+++ b/solution.py
@@ -15,6 +15,7 @@
 WIRE = BF16
 RIGHT, LEFT = 0, 1
 LAG = 6
+GAP = 4
 MESH = pl.DeviceIdType.MESH
 
 
@@ -144,6 +145,11 @@
     receives = {RIGHT: has_left, LEFT: has_right}
     near_end = {RIGHT: s == 1, LEFT: s == steps - 1}
     to_end = {RIGHT: s == steps - 1, LEFT: s == 1}
+    gap = {way: jnp.where(near_end[way], GAP if moved else 0, 0) for way in (RIGHT, LEFT)}
+    gathered_at = jnp.maximum(
+        jnp.where(s > 0, gap[RIGHT] + (s - 1) * cells, 0),
+        jnp.where(s < steps, gap[LEFT] + (steps - s - 1) * cells, 0),
+    )
 
     def to(way):
         return s + 1 if way == RIGHT else s - 1
@@ -302,7 +308,7 @@
         )
 
     def gather_own(b, way, there):
-        @pl.when(both(there, sends[way]))
+        @pl.when(jnp.logical_and(there, sends[way]))
         def _():
             def one(c, carry):
                 gather_copy(b, way, s, c, to(way)).start()
@@ -310,19 +316,18 @@
 
             lax.fori_loop(jnp.where(to_end[way], given[b], 0), cells, one, 0)
 
-    def gather_start(b, k):
-        gather_own(b, RIGHT, s == k)
-        gather_own(b, LEFT, s + k == steps)
-
     def gather_flat(b, begin, end):
         wait = min(5, cells - given[b])
 
         def one(i, carry):
-            k = lax.div(i, cells) + 1
-            c = lax.rem(i, cells)
-            whole = both(c >= given[b])
-            held = jnp.logical_or(whole, jnp.logical_not(ends))
-            for way, shard, here in ((LEFT, s + k, s + k < sts), (RIGHT, s - k, s >= k)):
+            for way in (LEFT, RIGHT):
+                m = i - gap[way]
+                k = lax.div(jnp.maximum(m, 0), cells) + 1
+                c = lax.rem(jnp.maximum(m, 0), cells)
+                shard = s - k if way == RIGHT else s + k
+                here = both(m >= 0, shard >= 0, shard < sts)
+                whole = c >= given[b]
+                held = jnp.logical_or(whole, jnp.logical_not(ends))
                 passed = jnp.logical_or(whole, jnp.logical_not(to_end[way]))
 
                 @pl.when(both(here, held))
@@ -333,22 +338,25 @@
                     def _():
                         gather_copy(b, way, shard, c, to(way)).start()
 
-            @pl.when(both(k == last_step, held))
+                if b + 1 < blocks:
+                    final = shard == (0 if way == RIGHT else steps)
+
+                    @pl.when(both(here, final, c == cells - 1))
+                    def _():
+                        gather_own(b + 1, way, True)
+
+            c = i - gathered_at
+
+            @pl.when(both(c >= jnp.where(ends, given[b], 0), c < cells))
             def _():
                 contract(b, c)
 
             if given[b]:
                 for way in (RIGHT, LEFT):
 
-                    @pl.when(both(k == last_step, near_end[way], c >= wait, c < wait + given[b]))
+                    @pl.when(both(near_end[way], c >= wait, c < wait + given[b]))
                     def _():
                         contract_near(b, way, c - wait)
-
-            if b + 1 < blocks:
-
-                @pl.when(c == cells - 1)
-                def _():
-                    gather_start(b + 1, k)
 
             return carry
 
@@ -752,21 +760,24 @@
     relayout()
     for i in range(2):
         near_start(0, i)
+    operator_end(0, 0)
+    operator_begin(1, 0)
     for b in range(1, blocks):
         start_load(b).wait()
         operator_begin(0, b)
     for b in range(blocks):
-        operator_end(0, b)
-        operator_begin(1, b)
-    for b in range(blocks):
         operator_end(1, b)
         if b == 0:
-            for k in range(sts):
-                gather_start(0, k)
+            for way in (RIGHT, LEFT):
+                gather_own(0, way, True)
             for i in range(2):
                 near_start(1, i)
+            for later in range(1, blocks):
+                operator_end(0, later)
+                operator_begin(1, later)
         if b == 1:
-            gather_start(1, 0)
+            for way in (RIGHT, LEFT):
+                gather_own(1, way, origin[way])
     for c in range(2, moved):
         for i in range(2):
             near_start(c, i)
@@ -831,10 +842,15 @@
     vmem = pl.BlockSpec(memory_space=pltpu.VMEM)
     smem = pl.BlockSpec(memory_space=pltpu.SMEM)
     anywhere = pl.BlockSpec(memory_space=pl.ANY)
+    far = pl.BlockSpec(memory_space=pltpu.HBM)
+
+    def hold(array):
+        return pltpu.with_memory_space_constraint(array, pltpu.HBM)
+
     return pl.pallas_call(
         partial(kernel, sizes),
         out_shape=jax.ShapeDtypeStruct((blocks, cells, width, nodes), BF16),
-        in_specs=[smem, smem, anywhere, anywhere, anywhere, vmem, vmem],
+        in_specs=[smem, smem, far, far, far, vmem, vmem],
         out_specs=anywhere,
         scratch_shapes=[
             pltpu.VMEM((blocks, cells, width, nodes), BF16),
@@ -885,16 +901,16 @@
             dma((blocks,)),
         ],
         compiler_params=pltpu.CompilerParams(
-            collective_id=0, has_side_effects=True, vmem_limit_bytes=60 * 1024 * 1024
+            collective_id=0, has_side_effects=True, vmem_limit_bytes=36 * 1024 * 1024
         ),
     )(
-        cell_scale,
+        hold(cell_scale),
         cell_count,
-        start_block,
-        jnp.transpose(resident, (2, 1, 0)),
-        stiffness,
-        potential,
-        face_index,
+        hold(start_block),
+        hold(jnp.transpose(resident, (2, 1, 0))),
+        hold(stiffness),
+        hold(potential),
+        hold(face_index),
     )
 
 

time: 93.6 us -> 92.3 us (0.986)
  local copies, waits for them, and re-layouts: 2.06 us -> 0.88 us
    unnamed x1, local copies, waits for them, and re-layouts: 2.06 us -> 0.88 us
where the time goes in v5:
time: 92.3 us; the launch traced here: 92.1 us
  Pallas kernels  90.5 us (98%)
    pallas_call x1, Pallas kernels, on_device(): pl.pallas_call(partial(kernel, sizes), out_shape=jax.ShapeDtypeStruct((bl...  90.5 us

profile of v5, /device:TPU:10, one launch (start us, length us, event | category | flops | bytes accessed | tf_op | source)
XLA Modules:
  0.0 92.1 jit_solution(4633402075126282528)
XLA Ops:
  0.7 90.5 %shard_map.73 = bf16[2,8,32,729]{3,2,1,0:T(8,128)(2,1)S(1)} custom-call(f32[8]{0:T(128)} %scale_ref.1, s32[1]{0:T(128)S(6)} %copy.9.count_ref, bf16[2,8,32,729]{3,2,1,0:T(8,128)(2,1)} %start_hbm.1, bf16[729,8,256]{2,1,0:T(8,128)(2,1)} %bitcast.1, bf16[729,729]{1,0:T(8,128)(2,1)} %stiff_hbm.1, f32[8,729]{1,0:T(8,128)} %pot_ref.1, s32[1,2,81]{2,1,0:T(2,128)} %face_ref.1), custom_call_target="tpu_custom_call" | custom-call | tf_op jit(solution)/shard_map/pallas_call | solution.py:850
  91.2 0.9 copy.10

commit v6 on v5

--- a/solution.py
+++ b/solution.py
@@ -127,13 +127,17 @@
     def res_load(at):
         return pltpu.make_async_copy(res_hbm.at[at], res_in.at[at], load_sem)
 
+    def res_start():
+        for at in cuts(nodes, 4):
+            res_load(at).start()
+
+    pl.when(ends)(res_start)
     start_load(0).start()
     for at in cuts(nodes, 2):
         stiff_load(at).start()
     for b in range(1, blocks):
         start_load(b).start()
-    for at in cuts(nodes, 4):
-        res_load(at).start()
+    pl.when(jnp.logical_not(ends))(res_start)
 
     origin = {RIGHT: s == 0, LEFT: s == steps}
     lag = {RIGHT: LAG * jnp.maximum(s - 1, 0), LEFT: LAG * jnp.maximum(steps - 1 - s, 0)}
@@ -754,12 +758,16 @@
 
     for b in range(blocks):
         part[b] = jnp.zeros(part.shape[1:], F32)
+    @pl.when(ends)
+    def _():
+        relayout()
+        meet()
+
+    for i in range(2):
+        near_start(0, i)
     start_load(0).wait()
     stiff_load(pl.ds(0, nodes)).wait()
-    operator_begin(0, 0, meet)
-    relayout()
-    for i in range(2):
-        near_start(0, i)
+    operator_begin(0, 0, lambda: pl.when(jnp.logical_not(ends))(meet))
     operator_end(0, 0)
     operator_begin(1, 0)
     for b in range(1, blocks):
@@ -772,6 +780,7 @@
                 gather_own(0, way, True)
             for i in range(2):
                 near_start(1, i)
+            pl.when(jnp.logical_not(ends))(relayout)
             for later in range(1, blocks):
                 operator_end(0, later)
                 operator_begin(1, later)

time: 92.3 us -> 91.2 us (0.988)
  Pallas kernels: 90.5 us -> 89.4 us
    pallas_call x1, Pallas kernels: 90.5 us -> 89.4 us  [on_device(): pl.pallas_call(partial(kernel, sizes), out_shape=jax.ShapeDtypeStruct((bl...]
where the time goes in v6:
time: 91.2 us; the launch traced here: 91 us
  Pallas kernels  89.4 us (98%)
    pallas_call x1, Pallas kernels, on_device(): pl.pallas_call(partial(kernel, sizes), out_shape=jax.ShapeDtypeStruct((bl...  89.4 us

profile of v6, /device:TPU:10, one launch (start us, length us, event | category | flops | bytes accessed | tf_op | source)
XLA Modules:
  0.0 91.0 jit_solution(9554726674437529791)
XLA Ops:
  0.7 89.4 %shard_map.73 = bf16[2,8,32,729]{3,2,1,0:T(8,128)(2,1)S(1)} custom-call(f32[8]{0:T(128)} %scale_ref.1, s32[1]{0:T(128)S(6)} %copy.9.count_ref, bf16[2,8,32,729]{3,2,1,0:T(8,128)(2,1)} %start_hbm.1, bf16[729,8,256]{2,1,0:T(8,128)(2,1)} %bitcast.1, bf16[729,729]{1,0:T(8,128)(2,1)} %stiff_hbm.1, f32[8,729]{1,0:T(8,128)} %pot_ref.1, s32[1,2,81]{2,1,0:T(2,128)} %face_ref.1), custom_call_target="tpu_custom_call" | custom-call | tf_op jit(solution)/shard_map/pallas_call | solution.py:859
  90.1 0.9 copy.10

commit v7 on v6

--- a/solution.py
+++ b/solution.py
@@ -141,6 +141,7 @@
 
     origin = {RIGHT: s == 0, LEFT: s == steps}
     lag = {RIGHT: LAG * jnp.maximum(s - 1, 0), LEFT: LAG * jnp.maximum(steps - 1 - s, 0)}
+    early = sts > 3
     done_at = jnp.maximum(
         jnp.where(s > 0, lag[RIGHT] + (steps - s) * cells, 0),
         jnp.where(s < steps, lag[LEFT] + s * cells, 0),
@@ -712,20 +713,25 @@
             def _():
                 retained[b, c] -= piece
 
-    def chain(turns, begin, end):
+    def chain(turns, begin, end, ready=None):
         def one(j, carry):
             for b, offset in turns:
                 chain_step(b, j + offset)
+            if ready is not None and early:
+                share_middle(ready, j - cells - 2)
             return carry
 
         lax.fori_loop(begin, end, one, 0)
 
+    def share_middle(b, c):
+        @pl.when(both(jnp.logical_not(ends), c >= 0, c < cells))
+        def _():
+            share_cell(b, c)
+            retain(b, c)
+
     def chain_step(b, j):
-        @pl.when(both(jnp.logical_not(ends), j < cells))
-        def _():
-            share_cell(b, j)
-            retain(b, j)
-
+        if b == 0 or not early:
+            share_middle(b, j)
         for way in (RIGHT, LEFT):
             m = j - lag[way]
             i = lax.div(jnp.maximum(m, 0), cells)
@@ -794,9 +800,9 @@
     half = cells // 2
     whole = steps * cells
     links = done_at + cells
-    over = 3 * cells // 4
-    cut_one = jnp.where(ends, done_at, cells // 2)
-    cut_two = jnp.where(ends, done_at + 2, cells)
+    over = cells - 2
+    cut_one = jnp.where(ends, done_at, cells - 1)
+    cut_two = jnp.where(ends, done_at, cells + 2)
     gather_flat(0, 0, whole)
     reduce_start(0)
     for b in range(blocks):
@@ -815,7 +821,7 @@
         coef_start(b)
         share_start(b)
         if previous:
-            chain([(b - 1, 0)], cut_two, links - over)
+            chain([(b - 1, 0)], cut_two, links - over, b)
             chain([(b - 1, links - over), (b, 0)], 0, over)
         if following:
             gather_flat(b + 1, cells, whole)

time: 91.2 us -> 90.8 us (level)
  no operation moved by 1% of the time
where the time goes in v7:
time: 90.8 us; the launch traced here: 90.6 us
  Pallas kernels  89.1 us (98%)
    pallas_call x1, Pallas kernels, on_device(): pl.pallas_call(partial(kernel, sizes), out_shape=jax.ShapeDtypeStruct((bl...  89.1 us

profile of v7, /device:TPU:10, one launch (start us, length us, event | category | flops | bytes accessed | tf_op | source)
XLA Modules:
  0.0 90.6 jit_solution(13922205044030977621)
XLA Ops:
  0.7 89.1 %shard_map.73 = bf16[2,8,32,729]{3,2,1,0:T(8,128)(2,1)S(1)} custom-call(f32[8]{0:T(128)} %scale_ref.1, s32[1]{0:T(128)S(6)} %copy.9.count_ref, bf16[2,8,32,729]{3,2,1,0:T(8,128)(2,1)} %start_hbm.1, bf16[729,8,256]{2,1,0:T(8,128)(2,1)} %bitcast.1, bf16[729,729]{1,0:T(8,128)(2,1)} %stiff_hbm.1, f32[8,729]{1,0:T(8,128)} %pot_ref.1, s32[1,2,81]{2,1,0:T(2,128)} %face_ref.1), custom_call_target="tpu_custom_call" | custom-call | tf_op jit(solution)/shard_map/pallas_call | solution.py:865
  89.7 0.9 copy.10

commit v8 on v7

--- a/solution.py
+++ b/solution.py
@@ -124,12 +124,17 @@
     def stiff_load(at):
         return pltpu.make_async_copy(stiff_hbm.at[at], stiff_ref.at[at], stiff_sem)
 
-    def res_load(at):
-        return pltpu.make_async_copy(res_hbm.at[at], res_in.at[at], load_sem)
+    chunks = nodes // face
+    parts = ((0, chunks // 2 + 1), (chunks // 2 + 1, chunks))
+
+    def res_load(i):
+        begin, end = parts[i]
+        at = pl.ds(begin * face, (end - begin) * face)
+        return pltpu.make_async_copy(res_hbm.at[at], res_in.at[at], load_sem.at[i])
 
     def res_start():
-        for at in cuts(nodes, 4):
-            res_load(at).start()
+        for i in range(2):
+            res_load(i).start()
 
     pl.when(ends)(res_start)
     start_load(0).start()
@@ -137,7 +142,6 @@
         stiff_load(at).start()
     for b in range(1, blocks):
         start_load(b).start()
-    pl.when(jnp.logical_not(ends))(res_start)
 
     origin = {RIGHT: s == 0, LEFT: s == steps}
     lag = {RIGHT: LAG * jnp.maximum(s - 1, 0), LEFT: LAG * jnp.maximum(steps - 1 - s, 0)}
@@ -198,9 +202,9 @@
     def mask(c):
         return live[c].astype(BF16)
 
-    def relayout():
-        res_load(pl.ds(0, nodes)).wait()
-        for chunk in range(nodes // face):
+    def relayout(i):
+        res_load(i).wait()
+        for chunk in range(*parts[i]):
             at = slice(chunk * face, (chunk + 1) * face)
             wide = res_in[at].astype(F32).reshape(face * cells, res)
             for h in range(res // 128):
@@ -234,16 +238,19 @@
     def operator_begin(step, b, meanwhile=None):
         field = partial(second if step else first, b)
         local[b] = dot_nn(field(None), stiff_ref[...])
+
+        def value(c, at):
+            potential = pot_ref[c : c + 1, at] * field(c)[:, at].astype(F32)
+            return scale[c] * local[b, rows_of(c), at] + potential
+
         last_tail = jnp.zeros((width, nodes - window), F32)
         for c in range(cells):
-            value = scale[c] * local[b, rows_of(c), :] + pot_ref[c : c + 1, :] * field(c).astype(F32)
-            local[b, rows_of(c), :] = value
-            last_tail = last_tail + last[c] * value[:, window:]
+            last_tail = last_tail + last[c] * value(c, slice(window, nodes))
         face_out[step, b, RIGHT] = dot_nn(
             last_tail, one_hot(0, window, nodes - window), lax.Precision.HIGHEST
         )
         face_out[step, b, LEFT] = dot_nn(
-            local[b, rows_of(0), :face], one_hot(1, 0, face), lax.Precision.HIGHEST
+            value(0, slice(0, face)), one_hot(1, 0, face), lax.Precision.HIGHEST
         )
         if meanwhile is not None:
             meanwhile()
@@ -254,6 +261,8 @@
                 face_copy(step, b, way).start()
 
             pending.append((there, partial(face_copy, step, b, way)))
+        for c in range(cells):
+            local[b, rows_of(c), :] = value(c, slice(0, nodes))
         for c in range(cells - 1):
             pair = live[c + 1]
             tail = local[b, rows_of(c), window:]
@@ -766,13 +775,15 @@
         part[b] = jnp.zeros(part.shape[1:], F32)
     @pl.when(ends)
     def _():
-        relayout()
+        relayout(0)
         meet()
 
-    for i in range(2):
-        near_start(0, i)
+    near_start(0, 0)
+    pl.when(ends)(partial(relayout, 1))
+    near_start(0, 1)
     start_load(0).wait()
     stiff_load(pl.ds(0, nodes)).wait()
+    pl.when(jnp.logical_not(ends))(res_start)
     operator_begin(0, 0, lambda: pl.when(jnp.logical_not(ends))(meet))
     operator_end(0, 0)
     operator_begin(1, 0)
@@ -786,7 +797,8 @@
                 gather_own(0, way, True)
             for i in range(2):
                 near_start(1, i)
-            pl.when(jnp.logical_not(ends))(relayout)
+            for i in range(2):
+                pl.when(jnp.logical_not(ends))(partial(relayout, i))
             for later in range(1, blocks):
                 operator_end(0, later)
                 operator_begin(1, later)
@@ -904,7 +916,7 @@
             dma((blocks,)),
             dma((blocks, sts)),
             dma((blocks, sts + 1, cells)),
-            dma,
+            dma((2,)),
             dma((blocks,)),
             dma,
             dma((blocks,)),

time: 90.8 us -> 90.4 us (level)
  no operation moved by 1% of the time
where the time goes in v8:
time: 90.4 us; the launch traced here: 90.2 us
  Pallas kernels  88.6 us (98%)
    pallas_call x1, Pallas kernels, on_device(): pl.pallas_call(partial(kernel, sizes), out_shape=jax.ShapeDtypeStruct((bl...  88.6 us

profile of v8, /device:TPU:10, one launch (start us, length us, event | category | flops | bytes accessed | tf_op | source)
XLA Modules:
  0.0 90.2 jit_solution(9392647367417178026)
XLA Ops:
  0.7 88.6 %shard_map.73 = bf16[2,8,32,729]{3,2,1,0:T(8,128)(2,1)S(1)} custom-call(f32[8]{0:T(128)} %scale_ref.1, s32[1]{0:T(128)S(6)} %copy.9.count_ref, bf16[2,8,32,729]{3,2,1,0:T(8,128)(2,1)} %start_hbm.1, bf16[729,8,256]{2,1,0:T(8,128)(2,1)} %bitcast.1, bf16[729,729]{1,0:T(8,128)(2,1)} %stiff_hbm.1, f32[8,729]{1,0:T(8,128)} %pot_ref.1, s32[1,2,81]{2,1,0:T(2,128)} %face_ref.1), custom_call_target="tpu_custom_call" | custom-call | tf_op jit(solution)/shard_map/pallas_call | solution.py:877
  89.3 0.9 copy.10

commit v9 on v8

--- a/solution.py
+++ b/solution.py
@@ -739,7 +739,9 @@
             retain(b, c)
 
     def chain_step(b, j):
-        if b == 0 or not early:
+        if b == 0 and early:
+            pl.when(j >= moved)(partial(share_middle, b, j))
+        elif not early:
             share_middle(b, j)
         for way in (RIGHT, LEFT):
             m = j - lag[way]
@@ -832,6 +834,9 @@
         coefficients(b)
         coef_start(b)
         share_start(b)
+        if b == 0 and early:
+            for c in range(moved):
+                share_middle(b, c)
         if previous:
             chain([(b - 1, 0)], cut_two, links - over, b)
             chain([(b - 1, links - over), (b, 0)], 0, over)

time: 90.4 us -> 90.4 us (level)
  no operation moved by 1% of the time
where the time goes in v9:
time: 90.4 us; the launch traced here: 90.2 us
  Pallas kernels  88.6 us (98%)
    pallas_call x1, Pallas kernels, on_device(): pl.pallas_call(partial(kernel, sizes), out_shape=jax.ShapeDtypeStruct((bl...  88.6 us

profile of v9, /device:TPU:10, one launch (start us, length us, event | category | flops | bytes accessed | tf_op | source)
XLA Modules:
  0.0 90.2 jit_solution(16223178204765454191)
XLA Ops:
  0.7 88.6 %shard_map.73 = bf16[2,8,32,729]{3,2,1,0:T(8,128)(2,1)S(1)} custom-call(f32[8]{0:T(128)} %scale_ref.1, s32[1]{0:T(128)S(6)} %copy.9.count_ref, bf16[2,8,32,729]{3,2,1,0:T(8,128)(2,1)} %start_hbm.1, bf16[729,8,256]{2,1,0:T(8,128)(2,1)} %bitcast.1, bf16[729,729]{1,0:T(8,128)(2,1)} %stiff_hbm.1, f32[8,729]{1,0:T(8,128)} %pot_ref.1, s32[1,2,81]{2,1,0:T(2,128)} %face_ref.1), custom_call_target="tpu_custom_call" | custom-call | tf_op jit(solution)/shard_map/pallas_call | solution.py:882
  89.3 0.9 copy.10
